TPU v7x, 128 devices: a whole 4x4x4 slice. The times are simulated.
128 devices in a mesh: gx: 8 (over y, z_lo), gy: 16 (over x, z_hi, core).
Axes of the slice: x: 4, y: 4, z: 4 (z_hi: 2, z_lo: 2; z = z_hi * 2 + z_lo), core: 2. Of those that a mesh axis runs over, the one named last changes fastest.
Arguments:
- coef: bfloat16 [131072, 512], P(('gx', 'gy')), may hold values from -6 to 6
- tables: bfloat16 [16, 512, 512], replicated, may hold values from -0.09375 to 0.09375
- leaf_level: int32 [131072], P(('gx', 'gy')), may hold values from 0 to 2
- inner_list: int32 [131072, 8], P(('gx', 'gy')), may hold values from 0 to 131071, as said below
- inner_class: int32 [131072, 8], P(('gx', 'gy')), may hold values from 0 to 15, as said below
- cross_pairs: int32 [3, 32768], P(None, ('gx', 'gy')), may hold values from 0 to 130175, as said below
Outputs:
- potential: float32 [131072, 512], P(('gx', 'gy'))
Inputs may be any that keep to these rules, and one draw needn't show every extreme that they name: `inner_list`: every entry of a row names a leaf of the same brick as the row's leaf; bricks are runs of 1024 leaves, brick number bx * 16 + by for brick column (bx, by). `inner_class`: the 8 classes of one row differ. `cross_pairs`: pair p belongs to owner brick p // 256; its target leaf is one of the first 128 leaves of the owner brick, its source one of the first 128 leaves of one of the up to eight bricks whose column differs from the owner's by at most one along x and y and which is not the owner; its class lies in 0 to 15.
All inputs are finite; a program needn't handle non-finite values.
Results may differ from a plain program's by a relative error of at most 0.0003.
Values may be sent and summed in bfloat16 or wider, within the bound.
A program may use at most 128 MiB of HBM per device.

v0:
```python
import jax
import jax.numpy as jnp
from jax import lax
from jax.sharding import PartitionSpec as P


def from_behind(block, axis, distance):
    devices = range(lax.axis_size(axis))
    route = [(i - distance, i) for i in devices if i - distance in devices]
    return lax.ppermute(block, axis, route)


def padded(block, sides, width):
    for axis, dim in sides:
        count = lax.axis_size(axis)
        forward = [(i, i + 1) for i in range(count - 1)]
        backward = [(target, source) for source, target in forward]
        low = lax.ppermute(
            lax.slice_in_dim(block, block.shape[dim] - width, None, axis=dim), axis, forward
        )
        high = lax.ppermute(lax.slice_in_dim(block, 0, width, axis=dim), axis, backward)
        block = jnp.concatenate([low, block, high], axis=dim)
    return block


def classed(rows, kind_ids, flat_tables, classes):
    onehot = (kind_ids[:, None] == jnp.arange(classes, dtype=jnp.int32)[None, :]).astype(rows.dtype)
    slots = (onehot[:, :, None] * rows[:, None, :]).reshape(rows.shape[0], classes * rows.shape[1])
    return jnp.dot(slots, flat_tables, preferred_element_type=jnp.float32)


def pick_rows(index, count, source_rows):
    picker = (index[:, None] == jnp.arange(count, dtype=jnp.int32)[None, :]).astype(
        source_rows.dtype
    )
    return jnp.dot(picker, source_rows, preferred_element_type=jnp.float32).astype(
        source_rows.dtype
    )


def add_rows(index, count, values, valid):
    picker = (
        (index[:, None] == jnp.arange(count, dtype=jnp.int32)[None, :]) & valid[:, None]
    ).astype(jnp.float32)
    return jnp.einsum(
        "pb,pw->bw",
        picker,
        values,
        precision=lax.Precision.HIGHEST,
        preferred_element_type=jnp.float32,
    )


def send_direct(piece, offset):
    return from_behind(piece, ("gx", "gy"), offset)


def body(coef, tables, leaf_level, inner_list, inner_class, cross_pairs):
    leaf_dev, width = coef.shape
    knear = inner_list.shape[1]
    classes = tables.shape[0]
    border = leaf_dev // 8
    count_y = lax.axis_size("gy")
    index_x = lax.axis_index("gx")
    index_y = lax.axis_index("gy")
    rank = index_x * count_y + index_y
    offset = rank * leaf_dev
    table_flat = tables.reshape(classes * width, width)
    table_back = jnp.transpose(tables, (0, 2, 1)).reshape(classes * width, width)
    halo_rows = padded(coef[:border][None, None], (("gx", 0), ("gy", 1)), 1)
    halo_rows = halo_rows.reshape(9 * border, width)
    local = inner_list - offset
    gathered = jnp.take(coef, local.reshape(-1), axis=0).reshape(leaf_dev, knear, width)
    inner_onehot = (
        inner_class[:, :, None] == jnp.arange(classes, dtype=jnp.int32)[None, None, :]
    ).astype(coef.dtype)
    slots = jnp.einsum(
        "lkc,lkw->lcw", inner_onehot, gathered, preferred_element_type=jnp.float32
    ).astype(jnp.bfloat16)
    near = jnp.dot(
        slots.reshape(leaf_dev, classes * width), table_flat, preferred_element_type=jnp.float32
    )
    target = cross_pairs[0] - offset
    source = cross_pairs[1]
    kind_ids = cross_pairs[2]
    all_valid = jnp.ones(target.shape, jnp.bool_)
    source_rank = source // leaf_dev
    place_x = source_rank // count_y - index_x + 1
    place_y = source_rank % count_y - index_y + 1
    place = (place_x * 3 + place_y) * border + source % leaf_dev
    source_rows = pick_rows(place, 9 * border, halo_rows)
    forward = classed(source_rows, kind_ids, table_flat, classes)
    border_sum = add_rows(target, border, forward, all_valid)
    target_rows = pick_rows(target, border, coef[:border])
    mirror = classed(target_rows, kind_ids, table_back, classes)
    outgoing = add_rows(place, 9 * border, mirror, all_valid).reshape(3, 3, border, width)
    returned = outgoing[1, 1]
    for step_x in range(3):
        for step_y in range(3):
            if step_x != 1 or step_y != 1:
                returned = returned + send_direct(
                    outgoing[step_x, step_y], (step_x - 1) * count_y + (step_y - 1)
                )
    border_sum = border_sum + returned
    near = near.at[:border].add(border_sum)
    scale = jnp.power(jnp.float32(0.25), leaf_level.astype(jnp.float32))
    return near * scale[:, None]


def solution(mesh):
    return jax.shard_map(
        body,
        mesh=mesh,
        in_specs=(
            P(("gx", "gy"), None),
            P(),
            P(("gx", "gy")),
            P(("gx", "gy"), None),
            P(("gx", "gy"), None),
            P(None, ("gx", "gy")),
        ),
        out_specs=P(("gx", "gy"), None),
        check_vma=False,
    )
```

profile of v0, /device:TPU:38, one launch (start us, length us, event | category | flops | bytes accessed | tf_op | source)
XLA Modules:
  0.0 162.8 jit_solution(17300051852179569149)
XLA Ops:
  0.0 0.9 slice_bitcast_fusion.9
  0.9 2.0 %collective-permute-start.1 = (bf16[1,1,128,512]{3,2,1,0:T(8,128)(2,1)S(1)}, bf16[1,1,128,512]{3,2,1,0:T(8,128)(2,1)}, u32[]{:S(2)}, u32[]{:S(2)}) collective-permute-start(bf16[1,1,128,512]{3,2,1,0:T(8,128)(2,1)S(1)} %slice_bitcast_fusion.9), channel_id=1, source_target_pairs={{16,0},{32,16},{48,32},{64,48},{80,64},{96,80},{112,96},{17,1},{33... | collective-permute-start | bytes 393224 | tf_op jit(solution)/shard_map/ppermute | solution.py:21
  2.9 4.7 %collective-permute-start = (bf16[1,1,128,512]{3,2,1,0:T(8,128)(2,1)S(1)}, bf16[1,1,128,512]{3,2,1,0:T(8,128)(2,1)}, u32[]{:S(2)}, u32[]{:S(2)}) collective-permute-start(bf16[1,1,128,512]{3,2,1,0:T(8,128)(2,1)S(1)} %slice_bitcast_fusion.9), channel_id=1, source_target_pairs={{0,16},{16,32},{32,48},{48,64},{64,80},{80,96},{96,112},{1,17},{17... | collective-permute-start | bytes 393224 | tf_op jit(solution)/shard_map/ppermute | solution.py:18
  7.7 0.8 fusion.46
  8.5 1.2 convolution_convert_fusion.1
  9.7 0.0 copy-start.7
  9.7 5.7 %fusion.19 = f32[256,512]{1,0:T(8,128)S(1)} fusion(bf16[16,512,512]{2,1,0:T(8,128)(2,1)} %param.9, bf16[256,512]{1,0:T(8,128)(2,1)S(1)} %convolution_convert_fusion.1, bf16[256,16]{0,1:T(8,128)(2,1)S(1)} %fusion.42), kind=kOutput, calls=%fused_computation.18 | convolution fusion | flops 2149580800 | bytes 9183232 | tf_op jit(solution)/shard_map/dot_general | solution.py:29
  15.5 0.0 copy-done.7
  15.5 0.0 copy-start.6
  15.5 0.0 copy-start
  15.5 1.2 fusion.24
  16.7 1.4 slice_bitcast_fusion.7
  18.1 1.9 %collective-permute-start.11 = (f32[128,512]{1,0:T(8,128)}, f32[128,512]{1,0:T(8,128)}, u32[]{:S(2)}, u32[]{:S(2)}) collective-permute-start(f32[128,512]{1,0:T(8,128)} %get-tuple-element.20), channel_id=1, source_target_pairs={{0,17},{1,18},{2,19},{3,20},{4,21},{5,22},{6,23},{7,24},{8,25},{9,... | collective-permute-start | bytes 786440 | tf_op jit(solution)/shard_map/ppermute | solution.py:10
  20.0 3.8 %collective-permute-start.10 = (f32[128,512]{1,0:T(8,128)}, f32[128,512]{1,0:T(8,128)}, u32[]{:S(2)}, u32[]{:S(2)}) collective-permute-start(f32[128,512]{1,0:T(8,128)} %get-tuple-element.21), channel_id=1, source_target_pairs={{0,16},{1,17},{2,18},{3,19},{4,20},{5,21},{6,22},{7,23},{8,24},{9,... | collective-permute-start | bytes 786440 | tf_op jit(solution)/shard_map/ppermute | solution.py:10
  23.8 4.2 %collective-permute-start.9 = (f32[128,512]{1,0:T(8,128)}, f32[128,512]{1,0:T(8,128)}, u32[]{:S(2)}, u32[]{:S(2)}) collective-permute-start(f32[128,512]{1,0:T(8,128)} %get-tuple-element.22), channel_id=1, source_target_pairs={{0,15},{1,16},{2,17},{3,18},{4,19},{5,20},{6,21},{7,22},{8,23},{9,... | collective-permute-start | bytes 786440 | tf_op jit(solution)/shard_map/ppermute | solution.py:10
  28.0 0.0 copy-done.6
  28.0 0.7 iota_compare_fusion.3
  28.8 3.1 %copy.14 = pred[1024,8,16]{2,1,0:T(8,128)(4,1)} copy(pred[1024,8,16]{0,2,1:T(8,128)(4,1)} %iota_compare_fusion.3) | data formatting | bytes 262144 | tf_op jit(solution)/shard_map/eq | solution.py:75
  31.9 1.4 compare_and_fusion
  33.3 1.8 %copy.13 = s32[1024,8]{1,0:T(8,128)} copy(s32[1024,8]{0,1:T(8,128)} %get-tuple-element.18) | data formatting | bytes 65536 | tf_op jit(solution)/shard_map/sub | solution.py:72
  35.0 1.9 %reshape.198 = s32[8192,1]{0,1:T(1,128)} reshape(s32[1024,8]{1,0:T(8,128)} %copy.13) | data formatting | bytes 65536 | tf_op jit(solution)/shard_map/reshape | solution.py:73
  37.0 0.8 compare_select_fusion
  37.8 0.6 broadcast_clamp_fusion
  38.4 0.0 copy-done
  38.4 36.4 %gather_fusion = bf16[8192,512]{1,0:T(8,128)(2,1)} fusion(bf16[1024,512]{1,0:T(8,128)(2,1)S(1)} %copy-done, s32[8192]{0:T(1024)} %broadcast_clamp_fusion), kind=kCustom, calls=%fused_computation | custom fusion | bytes 16809984 | tf_op jit(solution)/shard_map/jit(_take)/gather | solution.py:73
  74.8 0.3 copy.12
  75.1 11.8 %convolution_convert_fusion = bf16[1024,16,512]{2,1,0:T(8,128)(2,1)} fusion(pred[1024,8,16]{2,1,0:T(8,128)(4,1)} %copy.14, bf16[8192,512]{1,0:T(8,128)(2,1)} %gather_fusion, pred[1024,8]{1,0:T(8,128)(4,1)S(1)} %copy.12), kind=kOutput, calls=%fused_computation.3 | convolution fusion | flops 146800640 | bytes 25305088 | tf_op jit(solution)/shard_map/lkc,lkw->lcw/dot_general | solution.py:77
  86.9 0.0 collective-permute-done.1
  86.9 0.0 collective-permute-done
  86.9 0.0 slice-start
  86.9 1.2 pad_maximum_fusion.1
  88.1 0.0 copy-start.9
  88.1 0.0 copy-start.5
  88.1 0.0 copy-start.4
  88.1 0.0 slice-start.1
  88.1 4.0 %collective-permute-start.3 = (bf16[3,1,128,512]{3,2,1,0:T(8,128)(2,1)S(1)}, bf16[3,1,128,512]{3,2,1,0:T(8,128)(2,1)S(1)}, u32[]{:S(2)}, u32[]{:S(2)}) collective-permute-start(bf16[3,1,128,512]{3,2,1,0:T(8,128)(2,1)S(1)} %pad_maximum_fusion.1), channel_id=1, source_target_pairs={{1,0},{2,1},{3,2},{4,3},{5,4},{6,5},{7,6},{8,7},{9,8},{10,9},{11,1... | collective-permute-start | bytes 1179656 | tf_op jit(solution)/shard_map/ppermute | solution.py:21
  92.1 2.1 %collective-permute-start.2 = (bf16[3,1,128,512]{3,2,1,0:T(8,128)(2,1)S(1)}, bf16[3,1,128,512]{3,2,1,0:T(8,128)(2,1)S(1)}, u32[]{:S(2)}, u32[]{:S(2)}) collective-permute-start(bf16[3,1,128,512]{3,2,1,0:T(8,128)(2,1)S(1)} %pad_maximum_fusion.1), channel_id=1, source_target_pairs={{0,1},{1,2},{2,3},{3,4},{4,5},{5,6},{6,7},{7,8},{8,9},{9,10},{10,1... | collective-permute-start | bytes 1179656 | tf_op jit(solution)/shard_map/ppermute | solution.py:18
  94.2 30.1 %fusion.13 = f32[1024,512]{1,0:T(8,128)S(1)} fusion(bf16[16,512,512]{2,1,0:T(8,128)(2,1)} %param.9, bf16[1024,16,512]{2,1,0:T(8,128)(2,1)} %convolution_convert_fusion), kind=kOutput, calls=%fused_computation.16 | convolution fusion | flops 8589934592 | bytes 27262976 | tf_op jit(solution)/shard_map/dot_general | solution.py:80
  124.3 0.0 copy-done.9
  124.4 0.0 copy-start.3
  124.4 0.0 copy-start.2
  124.4 0.0 copy-start.1
  124.4 0.0 collective-permute-done.3
  124.4 0.0 copy-done.5
  124.4 4.3 %collective-permute-start.8 = (f32[128,512]{1,0:T(8,128)S(1)}, f32[128,512]{1,0:T(8,128)S(1)}, u32[]{:S(2)}, u32[]{:S(2)}) collective-permute-start(f32[128,512]{1,0:T(8,128)S(1)} %copy-done.5), channel_id=1, source_target_pairs={{0,1},{1,2},{2,3},{3,4},{4,5},{5,6},{6,7},{7,8},{8,9},{9,10},{10,1... | collective-permute-start | bytes 786440 | tf_op jit(solution)/shard_map/ppermute | solution.py:10
  128.7 0.0 collective-permute-done.2
  128.7 3.8 %collective-permute-start.7 = (f32[128,512]{1,0:T(8,128)S(1)}, f32[128,512]{1,0:T(8,128)S(1)}, u32[]{:S(2)}, u32[]{:S(2)}) collective-permute-start(f32[128,512]{1,0:T(8,128)S(1)} %copy-done.4), channel_id=1, source_target_pairs={{1,0},{2,1},{3,2},{4,3},{5,4},{6,5},{7,6},{8,7},{9,8},{10,9},{11,1... | collective-permute-start | bytes 786440 | tf_op jit(solution)/shard_map/ppermute | solution.py:10
  132.6 1.1 pad_maximum_fusion
  133.7 0.5 convolution_convert_fusion.2
  134.2 0.0 collective-permute-done.11
  134.2 1.9 %collective-permute-start.6 = (f32[128,512]{1,0:T(8,128)S(1)}, f32[128,512]{1,0:T(8,128)S(1)}, u32[]{:S(2)}, u32[]{:S(2)}) collective-permute-start(f32[128,512]{1,0:T(8,128)S(1)} %copy-done.3), channel_id=1, source_target_pairs={{15,0},{16,1},{17,2},{18,3},{19,4},{20,5},{21,6},{22,7},{23,8},{24... | collective-permute-start | bytes 786440 | tf_op jit(solution)/shard_map/ppermute | solution.py:10
  136.2 0.0 collective-permute-done.10
  136.2 0.0 copy-done.2
  136.2 3.5 %collective-permute-start.5 = (f32[128,512]{1,0:T(8,128)S(1)}, f32[128,512]{1,0:T(8,128)S(1)}, u32[]{:S(2)}, u32[]{:S(2)}) collective-permute-start(f32[128,512]{1,0:T(8,128)S(1)} %copy-done.2), channel_id=1, source_target_pairs={{16,0},{17,1},{18,2},{19,3},{20,4},{21,5},{22,6},{23,7},{24,8},{25... | collective-permute-start | bytes 786440 | tf_op jit(solution)/shard_map/ppermute | solution.py:10
  139.7 0.0 collective-permute-done.9
  139.7 2.1 %collective-permute-start.4 = (f32[128,512]{1,0:T(8,128)S(1)}, f32[128,512]{1,0:T(8,128)S(1)}, u32[]{:S(2)}, u32[]{:S(2)}) collective-permute-start(f32[128,512]{1,0:T(8,128)S(1)} %copy-done.1), channel_id=1, source_target_pairs={{17,0},{18,1},{19,2},{20,3},{21,4},{22,5},{23,6},{24,7},{25,8},{26... | collective-permute-start | bytes 786440 | tf_op jit(solution)/shard_map/ppermute | solution.py:10
  141.9 2.4 %fusion.16 = f32[256,512]{1,0:T(8,128)S(1)} fusion(bf16[16,512,512]{2,1,0:T(8,128)(2,1)S(1)} %bitcast.77, bf16[256,512]{1,0:T(8,128)(2,1)S(1)} %convolution_convert_fusion.2, bf16[256,16]{0,1:T(8,128)(2,1)S(1)} %copy-done.8), kind=kOutput, calls=%fused_computation.17 | convolution fusion | flops 2149580800 | bytes 9183232 | tf_op jit(solution)/shard_map/dot_general | solution.py:29
  144.3 0.0 collective-permute-done.8
  144.3 0.0 collective-permute-done.7
  144.3 0.0 collective-permute-done.6
  144.3 12.6 %collective-permute-done.5 = f32[128,512]{1,0:T(8,128)S(1)} collective-permute-done((f32[128,512]{1,0:T(8,128)S(1)}, f32[128,512]{1,0:T(8,128)S(1)}, u32[]{:S(2)}, u32[]{:S(2)}) %collective-permute-start.5) | collective-permute-done | bytes 262176 | tf_op jit(solution)/shard_map/ppermute | solution.py:10
  156.9 2.8 %collective-permute-done.4 = f32[128,512]{1,0:T(8,128)S(1)} collective-permute-done((f32[128,512]{1,0:T(8,128)S(1)}, f32[128,512]{1,0:T(8,128)S(1)}, u32[]{:S(2)}, u32[]{:S(2)}) %collective-permute-start.4) | collective-permute-done | bytes 262176 | tf_op jit(solution)/shard_map/ppermute | solution.py:10
  159.7 1.6 fusion.37
  161.3 1.5 broadcast_multiply_fusion
  (11 shorter events, 0.1 us)
Async XLA Ops:
  0.9 86.0 %collective-permute-start.1 = (bf16[1,1,128,512]{3,2,1,0:T(8,128)(2,1)S(1)}, bf16[1,1,128,512]{3,2,1,0:T(8,128)(2,1)}, u32[]{:S(2)}, u32[]{:S(2)}) collective-permute-start(bf16[1,1,128,512]{3,2,1,0:T(8,128)(2,1)S(1)} %slice_bitcast_fusion.9), channel_id=1, source_target_pairs={{16,0},{32,16},{48,32},{64,48},{80,64},{96,80},{112,96},{17,1},{33... | collective-permute-start | bytes 393224 | tf_op jit(solution)/shard_map/ppermute | solution.py:21
  2.9 84.0 %collective-permute-start = (bf16[1,1,128,512]{3,2,1,0:T(8,128)(2,1)S(1)}, bf16[1,1,128,512]{3,2,1,0:T(8,128)(2,1)}, u32[]{:S(2)}, u32[]{:S(2)}) collective-permute-start(bf16[1,1,128,512]{3,2,1,0:T(8,128)(2,1)S(1)} %slice_bitcast_fusion.9), channel_id=1, source_target_pairs={{0,16},{16,32},{32,48},{48,64},{64,80},{80,96},{96,112},{1,17},{17... | collective-permute-start | bytes 393224 | tf_op jit(solution)/shard_map/ppermute | solution.py:18
  9.7 5.8 %copy-start.7 = (bf16[256,16]{0,1:T(8,128)(2,1)}, bf16[256,16]{0,1:T(8,128)(2,1)S(1)}, u32[]{:S(2)}) copy-start(bf16[256,16]{0,1:T(8,128)(2,1)S(1)} %fusion.42) | copy-start | bytes 24580
  15.5 12.5 %copy-start.6 = (s32[1024,8]{0,1:T(8,128)S(1)}, s32[1024,8]{0,1:T(8,128)}, u32[]{:S(2)}) copy-start(s32[1024,8]{0,1:T(8,128)} %param.12) | copy-start | bytes 98308
  15.5 22.9 %copy-start = (bf16[1024,512]{1,0:T(8,128)(2,1)S(1)}, bf16[1024,512]{1,0:T(8,128)(2,1)}, u32[]{:S(2)}) copy-start(bf16[1024,512]{1,0:T(8,128)(2,1)} %param.8) | copy-start | bytes 3145732
  18.1 116.2 %collective-permute-start.11 = (f32[128,512]{1,0:T(8,128)}, f32[128,512]{1,0:T(8,128)}, u32[]{:S(2)}, u32[]{:S(2)}) collective-permute-start(f32[128,512]{1,0:T(8,128)} %get-tuple-element.20), channel_id=1, source_target_pairs={{0,17},{1,18},{2,19},{3,20},{4,21},{5,22},{6,23},{7,24},{8,25},{9,... | collective-permute-start | bytes 786440 | tf_op jit(solution)/shard_map/ppermute | solution.py:10
  20.0 116.2 %collective-permute-start.10 = (f32[128,512]{1,0:T(8,128)}, f32[128,512]{1,0:T(8,128)}, u32[]{:S(2)}, u32[]{:S(2)}) collective-permute-start(f32[128,512]{1,0:T(8,128)} %get-tuple-element.21), channel_id=1, source_target_pairs={{0,16},{1,17},{2,18},{3,19},{4,20},{5,21},{6,22},{7,23},{8,24},{9,... | collective-permute-start | bytes 786440 | tf_op jit(solution)/shard_map/ppermute | solution.py:10
  23.8 115.9 %collective-permute-start.9 = (f32[128,512]{1,0:T(8,128)}, f32[128,512]{1,0:T(8,128)}, u32[]{:S(2)}, u32[]{:S(2)}) collective-permute-start(f32[128,512]{1,0:T(8,128)} %get-tuple-element.22), channel_id=1, source_target_pairs={{0,15},{1,16},{2,17},{3,18},{4,19},{5,20},{6,21},{7,22},{8,23},{9,... | collective-permute-start | bytes 786440 | tf_op jit(solution)/shard_map/ppermute | solution.py:10
  86.9 55.0 %slice-start = ((s8[8388608]{0:T(1024)(128)(4,1)}), s8[4194304]{0:T(1024)(128)(4,1)S(1)}, s32[]{:S(2)}) async-start(s8[8388608]{0:T(1024)(128)(4,1)} %bitcast.76), calls=%async_computation | async-start | bytes 8388608
  88.1 36.3 %copy-start.9 = (s32[1024]{0:T(1024)S(1)}, s32[1024]{0:T(1024)}, u32[]{:S(2)}) copy-start(s32[1024]{0:T(1024)} %param.10) | copy-start | bytes 12292
  88.1 36.3 %copy-start.5 = (f32[128,512]{1,0:T(8,128)S(1)}, f32[128,512]{1,0:T(8,128)}, u32[]{:S(2)}) copy-start(f32[128,512]{1,0:T(8,128)} %get-tuple-element.23) | copy-start | bytes 786436
  88.1 40.6 %copy-start.4 = (f32[128,512]{1,0:T(8,128)S(1)}, f32[128,512]{1,0:T(8,128)}, u32[]{:S(2)}) copy-start(f32[128,512]{1,0:T(8,128)} %get-tuple-element.24) | copy-start | bytes 786436
  88.1 53.8 %slice-start.1 = ((s8[8388608]{0:T(1024)(128)(4,1)}), s8[4194304]{0:T(1024)(128)(4,1)S(1)}, s32[]{:S(2)}) async-start(s8[8388608]{0:T(1024)(128)(4,1)} %bitcast.76), calls=%async_computation.1 | async-start | bytes 8388608
  88.1 36.3 %collective-permute-start.3 = (bf16[3,1,128,512]{3,2,1,0:T(8,128)(2,1)S(1)}, bf16[3,1,128,512]{3,2,1,0:T(8,128)(2,1)S(1)}, u32[]{:S(2)}, u32[]{:S(2)}) collective-permute-start(bf16[3,1,128,512]{3,2,1,0:T(8,128)(2,1)S(1)} %pad_maximum_fusion.1), channel_id=1, source_target_pairs={{1,0},{2,1},{3,2},{4,3},{5,4},{6,5},{7,6},{8,7},{9,8},{10,9},{11,1... | collective-permute-start | bytes 1179656 | tf_op jit(solution)/shard_map/ppermute | solution.py:21
  92.1 36.6 %collective-permute-start.2 = (bf16[3,1,128,512]{3,2,1,0:T(8,128)(2,1)S(1)}, bf16[3,1,128,512]{3,2,1,0:T(8,128)(2,1)S(1)}, u32[]{:S(2)}, u32[]{:S(2)}) collective-permute-start(bf16[3,1,128,512]{3,2,1,0:T(8,128)(2,1)S(1)} %pad_maximum_fusion.1), channel_id=1, source_target_pairs={{0,1},{1,2},{2,3},{3,4},{4,5},{5,6},{6,7},{7,8},{8,9},{9,10},{10,1... | collective-permute-start | bytes 1179656 | tf_op jit(solution)/shard_map/ppermute | solution.py:18
  124.4 9.9 %copy-start.3 = (f32[128,512]{1,0:T(8,128)S(1)}, f32[128,512]{1,0:T(8,128)}, u32[]{:S(2)}) copy-start(f32[128,512]{1,0:T(8,128)} %get-tuple-element.25) | copy-start | bytes 786436
  124.4 11.8 %copy-start.2 = (f32[128,512]{1,0:T(8,128)S(1)}, f32[128,512]{1,0:T(8,128)}, u32[]{:S(2)}) copy-start(f32[128,512]{1,0:T(8,128)} %get-tuple-element.26) | copy-start | bytes 786436
  124.4 15.3 %copy-start.1 = (f32[128,512]{1,0:T(8,128)S(1)}, f32[128,512]{1,0:T(8,128)}, u32[]{:S(2)}) copy-start(f32[128,512]{1,0:T(8,128)} %get-tuple-element.19) | copy-start | bytes 786436
  124.4 17.5 %copy-start.8 = (bf16[256,16]{0,1:T(8,128)(2,1)S(1)}, bf16[256,16]{0,1:T(8,128)(2,1)}, u32[]{:S(2)}) copy-start(bf16[256,16]{0,1:T(8,128)(2,1)} %copy-done.7) | copy-start | bytes 24580
  124.4 19.9 %collective-permute-start.8 = (f32[128,512]{1,0:T(8,128)S(1)}, f32[128,512]{1,0:T(8,128)S(1)}, u32[]{:S(2)}, u32[]{:S(2)}) collective-permute-start(f32[128,512]{1,0:T(8,128)S(1)} %copy-done.5), channel_id=1, source_target_pairs={{0,1},{1,2},{2,3},{3,4},{4,5},{5,6},{6,7},{7,8},{8,9},{9,10},{10,1... | collective-permute-start | bytes 786440 | tf_op jit(solution)/shard_map/ppermute | solution.py:10
  128.7 15.6 %collective-permute-start.7 = (f32[128,512]{1,0:T(8,128)S(1)}, f32[128,512]{1,0:T(8,128)S(1)}, u32[]{:S(2)}, u32[]{:S(2)}) collective-permute-start(f32[128,512]{1,0:T(8,128)S(1)} %copy-done.4), channel_id=1, source_target_pairs={{1,0},{2,1},{3,2},{4,3},{5,4},{6,5},{7,6},{8,7},{9,8},{10,9},{11,1... | collective-permute-start | bytes 786440 | tf_op jit(solution)/shard_map/ppermute | solution.py:10
  134.2 10.1 %collective-permute-start.6 = (f32[128,512]{1,0:T(8,128)S(1)}, f32[128,512]{1,0:T(8,128)S(1)}, u32[]{:S(2)}, u32[]{:S(2)}) collective-permute-start(f32[128,512]{1,0:T(8,128)S(1)} %copy-done.3), channel_id=1, source_target_pairs={{15,0},{16,1},{17,2},{18,3},{19,4},{20,5},{21,6},{22,7},{23,8},{24... | collective-permute-start | bytes 786440 | tf_op jit(solution)/shard_map/ppermute | solution.py:10
  136.2 20.7 %collective-permute-start.5 = (f32[128,512]{1,0:T(8,128)S(1)}, f32[128,512]{1,0:T(8,128)S(1)}, u32[]{:S(2)}, u32[]{:S(2)}) collective-permute-start(f32[128,512]{1,0:T(8,128)S(1)} %copy-done.2), channel_id=1, source_target_pairs={{16,0},{17,1},{18,2},{19,3},{20,4},{21,5},{22,6},{23,7},{24,8},{25... | collective-permute-start | bytes 786440 | tf_op jit(solution)/shard_map/ppermute | solution.py:10
  139.7 20.0 %collective-permute-start.4 = (f32[128,512]{1,0:T(8,128)S(1)}, f32[128,512]{1,0:T(8,128)S(1)}, u32[]{:S(2)}, u32[]{:S(2)}) collective-permute-start(f32[128,512]{1,0:T(8,128)S(1)} %copy-done.1), channel_id=1, source_target_pairs={{17,0},{18,1},{19,2},{20,3},{21,4},{22,5},{23,6},{24,7},{25,8},{26... | collective-permute-start | bytes 786440 | tf_op jit(solution)/shard_map/ppermute | solution.py:10
where the time goes:
time: 164 us; the launch traced here: 163 us
  matrix products  54.6 us (33%)
  local copies, waits for them, and re-layouts  45.8 us (28%)
  starting transfers between devices  38.4 us (23%)
  waiting for transfers between devices  15.4 us (9%)
  other arithmetic  8.16 us (5%)
    gather x1, local copies, waits for them, and re-layouts, body(): jnp.take(coef, local.reshape(-1), axis=0).reshape(leaf_dev, knear, width)  36.4 us
    dot_general x1, matrix products, body(): jnp.dot(slots.reshape(leaf_dev, classes * width), table_flat, preferred_e...  30.1 us
    ppermute x8, starting transfers between devices, from_behind(): return lax.ppermute(block, axis, route)  25.6 us
    ppermute x8, waiting for transfers between devices, from_behind(): return lax.ppermute(block, axis, route)  15.4 us
    dot_general x1, matrix products, body(): jnp.einsum('lkc,lkw->lcw', inner_onehot, gathered, preferred_element_type...  11.8 us
    dot_general x2, matrix products, classed(): return jnp.dot(slots, flat_tables, preferred_element_type=jnp.float32)  8.12 us
    ppermute x2, starting transfers between devices, padded(): lax.ppermute(lax.slice_in_dim(block, block.shape[dim] - width, None, axis...  6.83 us
    ppermute x2, starting transfers between devices, padded(): lax.ppermute(lax.slice_in_dim(block, 0, width, axis=dim), axis, backward)  6 us
  transfers between devices with their start and end apart: 12, of which 2 were waited for; matrix products, arithmetic and copies ran while one was open for 64% of the time, Pallas kernels for 0%

commit v1 on v0

--- a/solution.py
+++ b/solution.py
@@ -1,6 +1,8 @@
 import jax
 import jax.numpy as jnp
 from jax import lax
+from jax.experimental import pallas as pl
+from jax.experimental.pallas import tpu as pltpu
 from jax.sharding import PartitionSpec as P
 
 
@@ -51,13 +53,70 @@
     )
 
 
+def inner_kernel(coef, tab, idx, out, y, acc):
+    c = pl.program_id(0)
+    leaf_dev = coef.shape[0]
+    rows = 4
+    base = c * (rows * leaf_dev)
+    half = leaf_dev // 2
+    for m in range(0, leaf_dev, half):
+        r = jnp.dot(coef[m : m + half, :], tab[0], preferred_element_type=jnp.float32)
+        for j in range(rows):
+            y[pl.ds(base + rows * m + j, half, stride=rows), :] = r[:, 128 * j : 128 * j + 128]
+
+    @pl.when(c == pl.num_programs(0) - 1)
+    def _():
+        unroll = 8
+
+        def step(i, _):
+            first = (i // 16) * 1024 + (i % 16) * unroll
+            for u in range(unroll):
+                total = None
+                for k in range(8):
+                    r = pl.multiple_of(idx[first + (k * 128 + u)], rows)
+                    v = y[pl.ds(r, rows), :]
+                    total = v if total is None else total + v
+                acc[pl.ds(pl.multiple_of(i * (unroll * rows) + u * rows, rows), rows), :] = total
+            return 0
+
+        lax.fori_loop(0, leaf_dev // unroll, step, 0)
+        for j in range(rows):
+            out[:, 128 * j : 128 * j + 128] = acc[pl.ds(j, leaf_dev, stride=rows), :]
+
+
+def inner_near(coef, tables, local, kinds):
+    leaf_dev, width = coef.shape
+    classes = tables.shape[0]
+    knear = local.shape[1]
+    rows = (kinds * leaf_dev + local).T * 4
+    rows = rows.reshape(knear, leaf_dev // 128, 128).transpose(1, 0, 2).reshape(-1)
+    return pl.pallas_call(
+        inner_kernel,
+        out_shape=jax.ShapeDtypeStruct((leaf_dev, width), jnp.float32),
+        grid=(classes,),
+        in_specs=[
+            pl.BlockSpec((leaf_dev, width), lambda c: (0, 0)),
+            pl.BlockSpec((1, width, width), lambda c: (c, 0, 0)),
+            pl.BlockSpec(memory_space=pltpu.SMEM),
+        ],
+        out_specs=pl.BlockSpec((leaf_dev, width), lambda c: (0, 0)),
+        scratch_shapes=[
+            pltpu.VMEM((classes * leaf_dev * 4, 128), jnp.float32),
+            pltpu.VMEM((leaf_dev * 4, 128), jnp.float32),
+        ],
+        compiler_params=pltpu.CompilerParams(vmem_limit_bytes=50 << 20),
+        cost_estimate=pl.CostEstimate(
+            flops=2 * leaf_dev * classes * width * width, bytes_accessed=12 << 20, transcendentals=0
+        ),
+    )(coef, tables, rows)
+
+
 def send_direct(piece, offset):
     return from_behind(piece, ("gx", "gy"), offset)
 
 
 def body(coef, tables, leaf_level, inner_list, inner_class, cross_pairs):
     leaf_dev, width = coef.shape
-    knear = inner_list.shape[1]
     classes = tables.shape[0]
     border = leaf_dev // 8
     count_y = lax.axis_size("gy")
@@ -70,16 +129,7 @@
     halo_rows = padded(coef[:border][None, None], (("gx", 0), ("gy", 1)), 1)
     halo_rows = halo_rows.reshape(9 * border, width)
     local = inner_list - offset
-    gathered = jnp.take(coef, local.reshape(-1), axis=0).reshape(leaf_dev, knear, width)
-    inner_onehot = (
-        inner_class[:, :, None] == jnp.arange(classes, dtype=jnp.int32)[None, None, :]
-    ).astype(coef.dtype)
-    slots = jnp.einsum(
-        "lkc,lkw->lcw", inner_onehot, gathered, preferred_element_type=jnp.float32
-    ).astype(jnp.bfloat16)
-    near = jnp.dot(
-        slots.reshape(leaf_dev, classes * width), table_flat, preferred_element_type=jnp.float32
-    )
+    near = inner_near(coef, tables, local, inner_class)
     target = cross_pairs[0] - offset
     source = cross_pairs[1]
     kind_ids = cross_pairs[2]

time: 164 us -> 104 us (0.63)
  the two profiles are of different devices: /device:TPU:38 before, /device:TPU:40 now
where the time goes in v1:
time: 104 us; the launch traced here: 103 us
  starting transfers between devices  46 us (44%)
  Pallas kernels  23.6 us (23%)
  matrix products  20.4 us (20%)
  waiting for transfers between devices  7.83 us (8%)
  other arithmetic  4.32 us (4%)
  local copies, waits for them, and re-layouts  1.1 us (1%)
    ppermute x8, starting transfers between devices, from_behind(): return lax.ppermute(block, axis, route)  37.5 us
    pallas_call x1, Pallas kernels, inner_near(): pl.pallas_call(inner_kernel, out_shape=jax.ShapeDtypeStruct((leaf_dev, wi...  23.6 us
    dot_general x2, matrix products, classed(): return jnp.dot(slots, flat_tables, preferred_element_type=jnp.float32)  17 us
    ppermute x2, waiting for transfers between devices, padded(): lax.ppermute(lax.slice_in_dim(block, 0, width, axis=dim), axis, backward)  7.81 us
    ppermute x2, starting transfers between devices, padded(): lax.ppermute(lax.slice_in_dim(block, block.shape[dim] - width, None, axis...  4.34 us
    ppermute x2, starting transfers between devices, padded(): lax.ppermute(lax.slice_in_dim(block, 0, width, axis=dim), axis, backward)  4.11 us
  transfers between devices with their start and end apart: 12, of which 2 were waited for; matrix products, arithmetic and copies ran while one was open for 11% of the time, Pallas kernels for 23%

profile of v1, /device:TPU:40, one launch (start us, length us, event | category | flops | bytes accessed | tf_op | source)
XLA Modules:
  0.0 103.5 jit_solution(16121344118165069365)
XLA Ops:
  0.0 0.9 slice_bitcast_fusion.9
  0.9 3.0 %collective-permute-start = (bf16[1,1,128,512]{3,2,1,0:T(8,128)(2,1)S(1)}, bf16[1,1,128,512]{3,2,1,0:T(8,128)(2,1)S(1)}, u32[]{:S(2)}, u32[]{:S(2)}) collective-permute-start(bf16[1,1,128,512]{3,2,1,0:T(8,128)(2,1)S(1)} %slice_bitcast_fusion.9), channel_id=1, source_target_pairs={{0,16},{16,32},{32,48},{48,64},{64,80},{80,96},{96,112},{1,17},{17... | collective-permute-start | bytes 393224 | tf_op jit(solution)/shard_map/ppermute | solution.py:20
  4.0 2.8 %collective-permute-start.1 = (bf16[1,1,128,512]{3,2,1,0:T(8,128)(2,1)S(1)}, bf16[1,1,128,512]{3,2,1,0:T(8,128)(2,1)S(1)}, u32[]{:S(2)}, u32[]{:S(2)}) collective-permute-start(bf16[1,1,128,512]{3,2,1,0:T(8,128)(2,1)S(1)} %slice_bitcast_fusion.9), channel_id=1, source_target_pairs={{16,0},{32,16},{48,32},{64,48},{80,64},{96,80},{112,96},{17,1},{33... | collective-permute-start | bytes 393224 | tf_op jit(solution)/shard_map/ppermute | solution.py:23
  6.8 0.8 fusion.34
  7.6 0.8 multiply_bitcast_fusion.idx
  8.4 0.1 fusion.28
  8.5 0.0 collective-permute-done
  8.5 3.2 %collective-permute-done.1 = bf16[1,1,128,512]{3,2,1,0:T(8,128)(2,1)S(1)} collective-permute-done((bf16[1,1,128,512]{3,2,1,0:T(8,128)(2,1)S(1)}, bf16[1,1,128,512]{3,2,1,0:T(8,128)(2,1)S(1)}, u32[]{:S(2)}, u32[]{:S(2)}) %collective-permute-start.1) | collective-permute-done | bytes 131104 | tf_op jit(solution)/shard_map/ppermute | solution.py:23
  11.8 1.3 %collective-permute-start.2 = (bf16[3,1,128,512]{3,2,1,0:T(8,128)(2,1)S(1)}, bf16[3,1,128,512]{3,2,1,0:T(8,128)(2,1)S(1)}, u32[]{:S(2)}, u32[]{:S(2)}) collective-permute-start(bf16[3,1,128,512]{3,2,1,0:T(8,128)(2,1)S(1)} %pad_maximum_fusion.1), channel_id=1, source_target_pairs={{0,1},{1,2},{2,3},{3,4},{4,5},{5,6},{6,7},{7,8},{8,9},{9,10},{10,1... | collective-permute-start | bytes 1179656 | tf_op jit(solution)/shard_map/ppermute | solution.py:20
  13.1 1.3 %collective-permute-start.3 = (bf16[3,1,128,512]{3,2,1,0:T(8,128)(2,1)S(1)}, bf16[3,1,128,512]{3,2,1,0:T(8,128)(2,1)S(1)}, u32[]{:S(2)}, u32[]{:S(2)}) collective-permute-start(bf16[3,1,128,512]{3,2,1,0:T(8,128)(2,1)S(1)} %pad_maximum_fusion.1), channel_id=1, source_target_pairs={{1,0},{2,1},{3,2},{4,3},{5,4},{6,5},{7,6},{8,7},{9,8},{10,9},{11,1... | collective-permute-start | bytes 1179656 | tf_op jit(solution)/shard_map/ppermute | solution.py:23
  14.4 1.2 %convolution_convert_fusion = bf16[256,512]{1,0:T(8,128)(2,1)S(1)} fusion(bf16[1024,512]{1,0:T(8,128)(2,1)} %coef.1, s32[256]{0:T(256)S(1)} %bitcast.71), kind=kOutput, calls=%fused_computation.9 | convolution fusion | flops 33718272 | bytes 394240 | tf_op jit(solution)/shard_map/dot_general | solution.py:38
  15.6 0.0 collective-permute-done.2
  15.6 4.6 %collective-permute-done.3 = bf16[3,1,128,512]{3,2,1,0:T(8,128)(2,1)S(1)} collective-permute-done((bf16[3,1,128,512]{3,2,1,0:T(8,128)(2,1)S(1)}, bf16[3,1,128,512]{3,2,1,0:T(8,128)(2,1)S(1)}, u32[]{:S(2)}, u32[]{:S(2)}) %collective-permute-start.3) | collective-permute-done | bytes 393248 | tf_op jit(solution)/shard_map/ppermute | solution.py:23
  20.2 0.1 pad_maximum_fusion
  20.3 0.5 convolution_convert_fusion.1
  20.9 0.9 broadcast_multiply_fusion.1
  21.8 8.4 %fusion.8 = f32[256,512]{1,0:T(8,128)S(1)} fusion(bf16[16,512,512]{2,1,0:T(8,128)(2,1)} %tab.1, bf16[256,16,512]{2,1,0:T(8,128)(2,1)S(1)} %get-tuple-element.26), kind=kOutput, calls=%fused_computation.8 | convolution fusion | flops 2147483648 | bytes 13107200 | tf_op jit(solution)/shard_map/dot_general | solution.py:31
  30.2 1.2 %fusion.13 = f32[1152,512]{1,0:T(8,128)S(1)} fusion(f32[256,512]{1,0:T(8,128)S(1)} %fusion.8, s32[256]{0:T(256)S(1)} %fusion.33), kind=kOutput, calls=%fused_computation.13 | convolution fusion | flops 1812234240 | bytes 2884608 | tf_op jit(solution)/shard_map/pb,pw->bw/dot_general | solution.py:47
  31.4 0.0 copy-start
  31.4 0.2 slice_bitcast_fusion.7
  31.6 3.8 %collective-permute-start.10 = (f32[128,512]{1,0:T(8,128)S(1)}, f32[128,512]{1,0:T(8,128)S(1)}, u32[]{:S(2)}, u32[]{:S(2)}) collective-permute-start(f32[128,512]{1,0:T(8,128)S(1)} %get-tuple-element.19), channel_id=1, source_target_pairs={{0,16},{1,17},{2,18},{3,19},{4,20},{5,21},{6,22},{7,23},{8,24},{9,... | collective-permute-start | bytes 786440 | tf_op jit(solution)/shard_map/ppermute | solution.py:12
  35.4 9.7 %collective-permute-start.11 = (f32[128,512]{1,0:T(8,128)S(1)}, f32[128,512]{1,0:T(8,128)S(1)}, u32[]{:S(2)}, u32[]{:S(2)}) collective-permute-start(f32[128,512]{1,0:T(8,128)S(1)} %get-tuple-element.18), channel_id=1, source_target_pairs={{0,17},{1,18},{2,19},{3,20},{4,21},{5,22},{6,23},{7,24},{8,25},{9,... | collective-permute-start | bytes 786440 | tf_op jit(solution)/shard_map/ppermute | solution.py:12
  45.1 0.0 copy-start.1
  45.1 1.9 %collective-permute-start.4 = (f32[128,512]{1,0:T(8,128)S(1)}, f32[128,512]{1,0:T(8,128)S(1)}, u32[]{:S(2)}, u32[]{:S(2)}) collective-permute-start(f32[128,512]{1,0:T(8,128)S(1)} %get-tuple-element.17), channel_id=1, source_target_pairs={{17,0},{18,1},{19,2},{20,3},{21,4},{22,5},{23,6},{24,7},{25,8},{26... | collective-permute-start | bytes 786440 | tf_op jit(solution)/shard_map/ppermute | solution.py:12
  47.0 0.0 copy-done
  47.0 23.6 %shard_map.64 = f32[1024,512]{1,0:T(8,128)S(1)} custom-call(bf16[1024,512]{1,0:T(8,128)(2,1)S(1)} %copy-done, bf16[16,512,512]{2,1,0:T(8,128)(2,1)} %tab.1, s32[8192]{0:T(1024)S(1)} %multiply_bitcast_fusion.idx), custom_call_target="tpu_custom_call" | custom-call | flops 8589934592 | bytes 12582912 | tf_op jit(solution)/shard_map/pallas_call | solution.py:93
  70.6 0.0 copy-done.1
  70.6 3.0 %collective-permute-start.5 = (f32[128,512]{1,0:T(8,128)S(1)}, f32[128,512]{1,0:T(8,128)S(1)}, u32[]{:S(2)}, u32[]{:S(2)}) collective-permute-start(f32[128,512]{1,0:T(8,128)S(1)} %get-tuple-element.24), channel_id=1, source_target_pairs={{16,0},{17,1},{18,2},{19,3},{20,4},{21,5},{22,6},{23,7},{24,8},{25... | collective-permute-start | bytes 786440 | tf_op jit(solution)/shard_map/ppermute | solution.py:12
  73.6 3.3 %collective-permute-start.6 = (f32[128,512]{1,0:T(8,128)S(1)}, f32[128,512]{1,0:T(8,128)S(1)}, u32[]{:S(2)}, u32[]{:S(2)}) collective-permute-start(f32[128,512]{1,0:T(8,128)S(1)} %get-tuple-element.23), channel_id=1, source_target_pairs={{15,0},{16,1},{17,2},{18,3},{19,4},{20,5},{21,6},{22,7},{23,8},{24... | collective-permute-start | bytes 786440 | tf_op jit(solution)/shard_map/ppermute | solution.py:12
  76.9 0.0 collective-permute-done.10
  76.9 4.4 %collective-permute-start.7 = (f32[128,512]{1,0:T(8,128)S(1)}, f32[128,512]{1,0:T(8,128)S(1)}, u32[]{:S(2)}, u32[]{:S(2)}) collective-permute-start(f32[128,512]{1,0:T(8,128)S(1)} %get-tuple-element.22), channel_id=1, source_target_pairs={{1,0},{2,1},{3,2},{4,3},{5,4},{6,5},{7,6},{8,7},{9,8},{10,9},{11,1... | collective-permute-start | bytes 786440 | tf_op jit(solution)/shard_map/ppermute | solution.py:12
  81.3 0.0 collective-permute-done.11
  81.3 1.9 %collective-permute-start.8 = (f32[128,512]{1,0:T(8,128)S(1)}, f32[128,512]{1,0:T(8,128)S(1)}, u32[]{:S(2)}, u32[]{:S(2)}) collective-permute-start(f32[128,512]{1,0:T(8,128)S(1)} %get-tuple-element.21), channel_id=1, source_target_pairs={{0,1},{1,2},{2,3},{3,4},{4,5},{5,6},{6,7},{7,8},{8,9},{9,10},{10,1... | collective-permute-start | bytes 786440 | tf_op jit(solution)/shard_map/ppermute | solution.py:12
  83.2 0.0 collective-permute-done.4
  83.2 9.6 %collective-permute-start.9 = (f32[128,512]{1,0:T(8,128)S(1)}, f32[128,512]{1,0:T(8,128)S(1)}, u32[]{:S(2)}, u32[]{:S(2)}) collective-permute-start(f32[128,512]{1,0:T(8,128)S(1)} %get-tuple-element.20), channel_id=1, source_target_pairs={{0,15},{1,16},{2,17},{3,18},{4,19},{5,20},{6,21},{7,22},{8,23},{9,... | collective-permute-start | bytes 786440 | tf_op jit(solution)/shard_map/ppermute | solution.py:12
  92.8 8.6 %fusion.5 = f32[256,512]{1,0:T(8,128)S(1)} fusion(bf16[16,512,512]{2,1,0:T(8,128)(2,1)} %tab.1, bf16[256,16,512]{2,1,0:T(8,128)(2,1)S(1)} %get-tuple-element.25), kind=kOutput, calls=%fused_computation.7 | convolution fusion | flops 2147483648 | bytes 13107200 | tf_op jit(solution)/shard_map/dot_general | solution.py:31
  101.4 0.0 collective-permute-done.5
  101.4 0.0 collective-permute-done.6
  101.4 0.0 collective-permute-done.7
  101.4 0.0 collective-permute-done.8
  101.4 0.0 collective-permute-done.9
  101.4 0.5 fusion.26
  101.9 1.5 %broadcast_multiply_fusion.2 = f32[1024,512]{1,0:T(8,128)} fusion(f32[1024,512]{1,0:T(8,128)S(1)} %fusion.26, f32[1024]{0:T(1024)S(1)} %convert_power_fusion), kind=kLoop, calls=%fused_computation.14 | loop fusion | flops 524288 | bytes 4198400 | tf_op jit(solution)/shard_map/mul | solution.py:157
  (3 shorter events, 0.1 us)
Async XLA Ops:
  0.9 7.6 %collective-permute-start = (bf16[1,1,128,512]{3,2,1,0:T(8,128)(2,1)S(1)}, bf16[1,1,128,512]{3,2,1,0:T(8,128)(2,1)S(1)}, u32[]{:S(2)}, u32[]{:S(2)}) collective-permute-start(bf16[1,1,128,512]{3,2,1,0:T(8,128)(2,1)S(1)} %slice_bitcast_fusion.9), channel_id=1, source_target_pairs={{0,16},{16,32},{32,48},{48,64},{64,80},{80,96},{96,112},{1,17},{17... | collective-permute-start | bytes 393224 | tf_op jit(solution)/shard_map/ppermute | solution.py:20
  4.0 7.8 %collective-permute-start.1 = (bf16[1,1,128,512]{3,2,1,0:T(8,128)(2,1)S(1)}, bf16[1,1,128,512]{3,2,1,0:T(8,128)(2,1)S(1)}, u32[]{:S(2)}, u32[]{:S(2)}) collective-permute-start(bf16[1,1,128,512]{3,2,1,0:T(8,128)(2,1)S(1)} %slice_bitcast_fusion.9), channel_id=1, source_target_pairs={{16,0},{32,16},{48,32},{64,48},{80,64},{96,80},{112,96},{17,1},{33... | collective-permute-start | bytes 393224 | tf_op jit(solution)/shard_map/ppermute | solution.py:23
  11.8 3.8 %collective-permute-start.2 = (bf16[3,1,128,512]{3,2,1,0:T(8,128)(2,1)S(1)}, bf16[3,1,128,512]{3,2,1,0:T(8,128)(2,1)S(1)}, u32[]{:S(2)}, u32[]{:S(2)}) collective-permute-start(bf16[3,1,128,512]{3,2,1,0:T(8,128)(2,1)S(1)} %pad_maximum_fusion.1), channel_id=1, source_target_pairs={{0,1},{1,2},{2,3},{3,4},{4,5},{5,6},{6,7},{7,8},{8,9},{9,10},{10,1... | collective-permute-start | bytes 1179656 | tf_op jit(solution)/shard_map/ppermute | solution.py:20
  13.1 7.1 %collective-permute-start.3 = (bf16[3,1,128,512]{3,2,1,0:T(8,128)(2,1)S(1)}, bf16[3,1,128,512]{3,2,1,0:T(8,128)(2,1)S(1)}, u32[]{:S(2)}, u32[]{:S(2)}) collective-permute-start(bf16[3,1,128,512]{3,2,1,0:T(8,128)(2,1)S(1)} %pad_maximum_fusion.1), channel_id=1, source_target_pairs={{1,0},{2,1},{3,2},{4,3},{5,4},{6,5},{7,6},{8,7},{9,8},{10,9},{11,1... | collective-permute-start | bytes 1179656 | tf_op jit(solution)/shard_map/ppermute | solution.py:23
  31.4 15.7 %copy-start = (bf16[1024,512]{1,0:T(8,128)(2,1)S(1)}, bf16[1024,512]{1,0:T(8,128)(2,1)}, u32[]{:S(2)}) copy-start(bf16[1024,512]{1,0:T(8,128)(2,1)} %coef.1) | copy-start | bytes 3145732
  31.6 45.3 %collective-permute-start.10 = (f32[128,512]{1,0:T(8,128)S(1)}, f32[128,512]{1,0:T(8,128)S(1)}, u32[]{:S(2)}, u32[]{:S(2)}) collective-permute-start(f32[128,512]{1,0:T(8,128)S(1)} %get-tuple-element.19), channel_id=1, source_target_pairs={{0,16},{1,17},{2,18},{3,19},{4,20},{5,21},{6,22},{7,23},{8,24},{9,... | collective-permute-start | bytes 786440 | tf_op jit(solution)/shard_map/ppermute | solution.py:12
  35.4 45.9 %collective-permute-start.11 = (f32[128,512]{1,0:T(8,128)S(1)}, f32[128,512]{1,0:T(8,128)S(1)}, u32[]{:S(2)}, u32[]{:S(2)}) collective-permute-start(f32[128,512]{1,0:T(8,128)S(1)} %get-tuple-element.18), channel_id=1, source_target_pairs={{0,17},{1,18},{2,19},{3,20},{4,21},{5,22},{6,23},{7,24},{8,25},{9,... | collective-permute-start | bytes 786440 | tf_op jit(solution)/shard_map/ppermute | solution.py:12
  45.1 25.5 %copy-start.1 = (s32[1024]{0:T(1024)S(1)}, s32[1024]{0:T(1024)}, u32[]{:S(2)}) copy-start(s32[1024]{0:T(1024)} %param.10) | copy-start | bytes 12292
  45.1 38.1 %collective-permute-start.4 = (f32[128,512]{1,0:T(8,128)S(1)}, f32[128,512]{1,0:T(8,128)S(1)}, u32[]{:S(2)}, u32[]{:S(2)}) collective-permute-start(f32[128,512]{1,0:T(8,128)S(1)} %get-tuple-element.17), channel_id=1, source_target_pairs={{17,0},{18,1},{19,2},{20,3},{21,4},{22,5},{23,6},{24,7},{25,8},{26... | collective-permute-start | bytes 786440 | tf_op jit(solution)/shard_map/ppermute | solution.py:12
  70.6 30.8 %collective-permute-start.5 = (f32[128,512]{1,0:T(8,128)S(1)}, f32[128,512]{1,0:T(8,128)S(1)}, u32[]{:S(2)}, u32[]{:S(2)}) collective-permute-start(f32[128,512]{1,0:T(8,128)S(1)} %get-tuple-element.24), channel_id=1, source_target_pairs={{16,0},{17,1},{18,2},{19,3},{20,4},{21,5},{22,6},{23,7},{24,8},{25... | collective-permute-start | bytes 786440 | tf_op jit(solution)/shard_map/ppermute | solution.py:12
  73.6 27.8 %collective-permute-start.6 = (f32[128,512]{1,0:T(8,128)S(1)}, f32[128,512]{1,0:T(8,128)S(1)}, u32[]{:S(2)}, u32[]{:S(2)}) collective-permute-start(f32[128,512]{1,0:T(8,128)S(1)} %get-tuple-element.23), channel_id=1, source_target_pairs={{15,0},{16,1},{17,2},{18,3},{19,4},{20,5},{21,6},{22,7},{23,8},{24... | collective-permute-start | bytes 786440 | tf_op jit(solution)/shard_map/ppermute | solution.py:12
  76.9 24.5 %collective-permute-start.7 = (f32[128,512]{1,0:T(8,128)S(1)}, f32[128,512]{1,0:T(8,128)S(1)}, u32[]{:S(2)}, u32[]{:S(2)}) collective-permute-start(f32[128,512]{1,0:T(8,128)S(1)} %get-tuple-element.22), channel_id=1, source_target_pairs={{1,0},{2,1},{3,2},{4,3},{5,4},{6,5},{7,6},{8,7},{9,8},{10,9},{11,1... | collective-permute-start | bytes 786440 | tf_op jit(solution)/shard_map/ppermute | solution.py:12
  81.3 20.1 %collective-permute-start.8 = (f32[128,512]{1,0:T(8,128)S(1)}, f32[128,512]{1,0:T(8,128)S(1)}, u32[]{:S(2)}, u32[]{:S(2)}) collective-permute-start(f32[128,512]{1,0:T(8,128)S(1)} %get-tuple-element.21), channel_id=1, source_target_pairs={{0,1},{1,2},{2,3},{3,4},{4,5},{5,6},{6,7},{7,8},{8,9},{9,10},{10,1... | collective-permute-start | bytes 786440 | tf_op jit(solution)/shard_map/ppermute | solution.py:12
  83.2 18.2 %collective-permute-start.9 = (f32[128,512]{1,0:T(8,128)S(1)}, f32[128,512]{1,0:T(8,128)S(1)}, u32[]{:S(2)}, u32[]{:S(2)}) collective-permute-start(f32[128,512]{1,0:T(8,128)S(1)} %get-tuple-element.20), channel_id=1, source_target_pairs={{0,15},{1,16},{2,17},{3,18},{4,19},{5,20},{6,21},{7,22},{8,23},{9,... | collective-permute-start | bytes 786440 | tf_op jit(solution)/shard_map/ppermute | solution.py:12

commit v2 on v0

v2 whole, which is shorter than its diff:
```python
import functools

import jax
import jax.numpy as jnp
from jax import lax
from jax.experimental import pallas as pl
from jax.experimental.pallas import tpu as pltpu
from jax.sharding import PartitionSpec as P

MESH = pl.DeviceIdType.MESH
ROWS = 4
ROOM = 64
STEPS = [(dx, dy) for dx in (-1, 0, 1) for dy in (-1, 0, 1) if (dx, dy) != (0, 0)]


def dot(a, b):
    return jnp.dot(a, b, preferred_element_type=jnp.float32)


def dot_t(a, b):
    return lax.dot_general(a, b, (((1,), (1,)), ((), ())), preferred_element_type=jnp.float32)


def split(z):
    high = z.astype(jnp.bfloat16)
    return high, (z - high.astype(jnp.float32)).astype(jnp.bfloat16)


def one_hot(mask):
    return jnp.where(mask, 1.0, 0.0).astype(jnp.bfloat16)


def iota(shape, dim):
    return lax.broadcasted_iota(jnp.int32, shape, dim)


def near_kernel(
    size_x,
    size_y,
    coef,
    pairs,
    idx,
    tabs_hbm,
    out,
    border_out,
    most_out,
    halo_out,
    lists_out,
    tabs,
    y,
    acc,
    halo,
    lists,
    g,
    back,
    x_m,
    x_f,
    z_m,
    z_f,
    tab_sem,
    send_sem,
    recv_sem,
    save_sem,
):
    leaf_dev, width = coef.shape
    classes = tabs.shape[0]
    border = leaf_dev // 8
    own = pairs.shape[1]
    my_x, my_y = lax.axis_index("gx"), lax.axis_index("gy")

    def table_copy(c):
        return pltpu.make_async_copy(tabs_hbm.at[c], tabs.at[c], tab_sem.at[c])

    for c in range(classes):
        table_copy(c).start()

    def neighbour(dx, dy):
        return lax.rem(my_x + dx + size_x, size_x), lax.rem(my_y + dy + size_y, size_y)

    barrier = pltpu.get_barrier_semaphore()
    for dx, dy in STEPS:
        pl.semaphore_signal(barrier, inc=1, device_id=neighbour(dx, dy), device_id_type=MESH)
    pl.semaphore_wait(barrier, len(STEPS))
    copies = []
    for there, (dx, dy) in enumerate(STEPS):
        here = len(STEPS) - 1 - there
        for part, (source, target) in enumerate(
            ((pairs, lists.at[here]), (coef.at[pl.ds(0, border)], halo.at[pl.ds(here * border, border)]))
        ):
            copy = pltpu.make_async_remote_copy(
                src_ref=source,
                dst_ref=target,
                send_sem=send_sem.at[part, there],
                recv_sem=recv_sem.at[part, here],
                device_id=neighbour(dx, dy),
                device_id_type=MESH,
            )
            copy.start()
            copies.append(copy)

    def tables_step(i, _):
        for u in range(2):
            c = i * 2 + u
            table_copy(c).wait()
            half = leaf_dev // 2
            for m in range(0, leaf_dev, half):
                r = dot(coef[m : m + half, :], tabs[c])
                for j in range(ROWS):
                    y[pl.ds(c * (ROWS * leaf_dev) + (ROWS * m + j), half, stride=ROWS), :] = r[
                        :, 128 * j : 128 * j + 128
                    ]
        return 0

    lax.fori_loop(0, classes // 2, tables_step, 0)

    for copy in copies:
        copy.wait()
    saves = [
        pltpu.make_async_copy(halo, halo_out, save_sem.at[0]),
        pltpu.make_async_copy(lists, lists_out, save_sem.at[1]),
    ]
    for save in saves:
        save.start()

    target, source, kind = pairs[0:1, :], pairs[1:2, :], pairs[2:3, :]
    rank = my_x * size_y + my_y
    home = source // leaf_dev
    place = (home // size_y - my_x + 1) * 3 + (home % size_y - my_y + 1)
    place = jnp.where(place > 4, place - 1, place)
    row = place * border + source % leaf_dev
    line = iota((128, own), 0)
    columns = jnp.transpose(jnp.where(line == 0, row, kind).astype(jnp.float32))
    row_col = columns[:, 0:1].astype(jnp.int32)
    kind_col = columns[:, 1:2].astype(jnp.int32)
    picker = one_hot(iota((own, halo.shape[0]), 1) == row_col)
    x_f[...] = dot(picker, halo[...]).astype(jnp.bfloat16)

    slots = classes * ROOM
    earlier = one_hot(iota((own, own), 0) < iota((own, own), 1))
    back[...] = jnp.zeros_like(back)

    def list_step(o, carry):
        before, most = carry
        nine = jnp.where(o >= 4, o + 1, o)
        there_x = lax.rem(my_x + nine // 3 - 1 + size_x, size_x)
        there_y = lax.rem(my_y + nine % 3 - 1 + size_y, size_y)
        from_leaf = lists[o, 0:1, :] - (there_x * size_y + there_y) * leaf_dev
        to_leaf = lists[o, 1:2, :] - rank * leaf_dev
        o_kind = lists[o, 2:3, :]
        here = (to_leaf >= 0) & (to_leaf < border)
        kinds = one_hot((iota((classes, own), 0) == o_kind) & here)
        ahead = dot(kinds, earlier) + before
        hits = kinds.astype(jnp.float32)
        place_in = jnp.sum(ahead * hits, axis=0, keepdims=True).astype(jnp.int32)
        most = jnp.maximum(most, jnp.where(here, place_in, 0))
        slot = jnp.where(here & (place_in < ROOM), o_kind * ROOM + place_in, -1)
        e = one_hot(iota((slots, own), 0) == slot)
        lines = iota((2 * border, own), 0)
        w = one_hot(lines == jnp.where(lines < border, from_leaf, to_leaf + border))
        both = dot_t(e, w)
        g[:, pl.ds(pl.multiple_of(o * border, border), border)] = both[:, :border].astype(jnp.bfloat16)
        back[...] += both[:, border:]
        return before + jnp.sum(hits, axis=1, keepdims=True), most

    _, most = lax.fori_loop(
        0,
        len(STEPS),
        list_step,
        (jnp.zeros((classes, 1), jnp.float32), jnp.zeros((1, own), jnp.int32)),
    )
    most_out[...] = jnp.broadcast_to(most, most_out.shape)
    x_m[...] = dot(g[...], halo[...]).astype(jnp.bfloat16)
    z_f[...] = jnp.zeros_like(z_f)

    share = leaf_dev // classes

    def class_step(c, _):
        table = tabs[c]
        rows = jnp.where(kind_col == c, x_f[...].astype(jnp.float32), 0.0).astype(jnp.bfloat16)
        z_f[...] += dot(rows, table)
        at = pl.ds(pl.multiple_of(c * ROOM, ROOM), ROOM)
        z_m[at, :] = dot_t(x_m[at, :], table)
        first = (c // 2) * 1024 + (c % 2) * share
        for u in range(share):
            total = None
            for k in range(8):
                r = idx[first + (k * 128 + u)]
                v = y[pl.ds(r, ROWS), :]
                total = v if total is None else total + v
            acc[pl.ds(pl.multiple_of(c * (share * ROWS) + u * ROWS, ROWS), ROWS), :] = total
        return 0

    lax.fori_loop(0, classes, class_step, 0)

    to_target = one_hot(iota((border, own), 0) == target - rank * leaf_dev)
    to_source = jnp.transpose(back[...]).astype(jnp.bfloat16)
    border_sum = None
    for picks, z in ((to_target, z_f[...]), (to_source, z_m[...])):
        for part in split(z):
            term = dot(picks, part)
            border_sum = term if border_sum is None else border_sum + term
    border_out[...] = border_sum
    for j in range(ROWS):
        out[:, 128 * j : 128 * j + 128] = acc[pl.ds(j, leaf_dev, stride=ROWS), :]
    for save in saves:
        save.wait()


def near_parts(size_x, size_y, coef, tables, pairs, rows):
    leaf_dev, width = coef.shape
    classes = tables.shape[0]
    border = leaf_dev // 8
    own = pairs.shape[1]
    places = len(STEPS)
    slots = classes * ROOM
    vmem = pl.BlockSpec(memory_space=pltpu.VMEM)
    hbm = pl.BlockSpec(memory_space=pl.ANY)
    return pl.pallas_call(
        functools.partial(near_kernel, size_x, size_y),
        out_shape=(
            jax.ShapeDtypeStruct((leaf_dev, width), jnp.float32),
            jax.ShapeDtypeStruct((border, width), jnp.float32),
            jax.ShapeDtypeStruct((8, own), jnp.int32),
            jax.ShapeDtypeStruct((places * border, width), jnp.bfloat16),
            jax.ShapeDtypeStruct((places, *pairs.shape), jnp.int32),
        ),
        in_specs=[vmem, vmem, pl.BlockSpec(memory_space=pltpu.SMEM), hbm],
        out_specs=(vmem, vmem, vmem, hbm, hbm),
        scratch_shapes=[
            pltpu.VMEM((classes, width, width), jnp.bfloat16),
            pltpu.VMEM((classes * leaf_dev * ROWS, 128), jnp.float32),
            pltpu.VMEM((leaf_dev * ROWS, 128), jnp.float32),
            pltpu.VMEM((places * border, width), jnp.bfloat16),
            pltpu.VMEM((places, *pairs.shape), jnp.int32),
            pltpu.VMEM((slots, places * border), jnp.bfloat16),
            pltpu.VMEM((slots, border), jnp.float32),
            pltpu.VMEM((slots, width), jnp.bfloat16),
            pltpu.VMEM((own, width), jnp.bfloat16),
            pltpu.VMEM((slots, width), jnp.float32),
            pltpu.VMEM((own, width), jnp.float32),
            pltpu.SemaphoreType.DMA((classes,)),
            pltpu.SemaphoreType.DMA((2, places)),
            pltpu.SemaphoreType.DMA((2, places)),
            pltpu.SemaphoreType.DMA((2,)),
        ],
        compiler_params=pltpu.CompilerParams(
            collective_id=0, has_side_effects=True, vmem_limit_bytes=60 << 20
        ),
    )(coef, pairs, rows, tables)


def add_rows(index, count, values, valid):
    picker = (
        (index[:, None] == jnp.arange(count, dtype=jnp.int32)[None, :]) & valid[:, None]
    ).astype(jnp.float32)
    return jnp.einsum(
        "pb,pw->bw",
        picker,
        values,
        precision=lax.Precision.HIGHEST,
        preferred_element_type=jnp.float32,
    )


def general_border(size_x, size_y, leaf_dev, halo, lists, pairs, tables):
    classes, width, _ = tables.shape
    border = leaf_dev // 8
    index_x, index_y = lax.axis_index("gx"), lax.axis_index("gy")
    rank = index_x * size_y + index_y
    home = pairs[1] // leaf_dev
    place = (home // size_y - index_x + 1) * 3 + (home % size_y - index_y + 1)
    place = jnp.where(place > 4, place - 1, place)
    picked = jnp.take(halo, place * border + pairs[1] % leaf_dev, axis=0)

    def products(rows, kinds, contract):
        def one(c, total):
            here = jnp.where((kinds == c)[:, None], rows, jnp.zeros_like(rows))
            return total + lax.dot_general(
                here, tables[c], (((1,), (contract,)), ((), ())), preferred_element_type=jnp.float32
            )

        return lax.fori_loop(0, classes, one, jnp.zeros((rows.shape[0], width), jnp.float32))

    everywhere = jnp.ones(pairs[0].shape, jnp.bool_)
    total = add_rows(pairs[0] - rank * leaf_dev, border, products(picked, pairs[2], 0), everywhere)

    def one_place(o, total):
        nine = jnp.where(o >= 4, o + 1, o)
        there_x = lax.rem(index_x + nine // 3 - 1 + size_x, size_x)
        there_y = lax.rem(index_y + nine % 3 - 1 + size_y, size_y)
        there = (there_x * size_y + there_y) * leaf_dev
        here = lists[o, 1] - rank * leaf_dev
        valid = (here >= 0) & (here < border)
        rows = jnp.take(halo, o * border + jnp.clip(lists[o, 0] - there, 0, border - 1), axis=0)
        return total + add_rows(here, border, products(rows, lists[o, 2], 1), valid)

    return lax.fori_loop(0, len(STEPS), one_place, total)


def body(coef, tables, leaf_level, inner_list, inner_class, cross_pairs):
    leaf_dev, width = coef.shape
    knear = inner_list.shape[1]
    border = leaf_dev // 8
    size_x, size_y = lax.axis_size("gx"), lax.axis_size("gy")
    rank = lax.axis_index("gx") * size_y + lax.axis_index("gy")
    rows = (inner_class * leaf_dev + (inner_list - rank * leaf_dev)).T * ROWS
    rows = rows.reshape(knear, leaf_dev // 128, 128).transpose(1, 0, 2).reshape(-1)
    near, border_sum, most, halo, lists = near_parts(
        size_x, size_y, coef, tables, cross_pairs, rows
    )
    border_sum = lax.cond(
        jnp.max(most) >= ROOM,
        lambda: general_border(size_x, size_y, leaf_dev, halo, lists, cross_pairs, tables),
        lambda: border_sum,
    )
    near = near.at[:border].add(border_sum)
    scale = jnp.power(jnp.float32(0.25), leaf_level.astype(jnp.float32))
    return near * scale[:, None]


def solution(mesh):
    return jax.shard_map(
        body,
        mesh=mesh,
        in_specs=(
            P(("gx", "gy"), None),
            P(),
            P(("gx", "gy")),
            P(("gx", "gy"), None),
            P(("gx", "gy"), None),
            P(None, ("gx", "gy")),
        ),
        out_specs=P(("gx", "gy"), None),
        check_vma=False,
    )
```

time: 164 us -> 56.1 us (0.34)
  the two profiles are of different devices: /device:TPU:38 before, /device:TPU:1 now
where the time goes in v2:
time: 56.1 us; the launch traced here: 55.8 us
  Pallas kernels  47.4 us (84%)
  other arithmetic  7.62 us (14%)
  between operations  0.69 us (1%)
    pallas_call x1, Pallas kernels, near_parts(): pl.pallas_call(functools.partial(near_kernel, size_x, size_y), out_shape=...  47.4 us
    mul x1, other arithmetic, body(): return near * scale[:, None]  3.12 us
    scatter-add x1, other arithmetic, body(): near = near.at[:border].add(border_sum)  1.76 us
    reshape x1, other arithmetic, body(): rows.reshape(knear, leaf_dev // 128, 128).transpose(1, 0, 2).reshape(-1)  1.4 us
    reduce_max x1, other arithmetic, body(): jnp.max(most) >= ROOM  1.34 us

profile of v2, /device:TPU:1, one launch (start us, length us, event | category | flops | bytes accessed | tf_op | source)
XLA Modules:
  0.0 55.8 jit_solution(7867519538580512892)
XLA Ops:
  0.0 1.4 %multiply_bitcast_fusion.idx = s32[8192]{0:T(1024)} fusion(s32[1024,8]{0,1:T(8,128)} %param.21, s32[1024,8]{0,1:T(8,128)} %param.22, s32[]{:T(128)S(6)} %mul.93), kind=kLoop, calls=%fused_computation.57 | loop fusion | flops 32768 | bytes 98308 | tf_op jit(solution)/shard_map/reshape | solution.py:307
  1.4 0.0 copy-start
  1.4 47.4 %shard_map.64 = (f32[1024,512]{1,0:T(8,128)}, f32[128,512]{1,0:T(8,128)}, s32[8,256]{1,0:T(8,128)}, bf16[1024,512]{1,0:T(8,128)(2,1)S(1)}, s32[8,3,256]{2,1,0:T(4,128)S(1)}) custom-call(bf16[1024,512]{1,0:T(8,128)(2,1)} %coef.1, s32[3,256]{1,0:T(4,128)} %pairs.1, s32[8192]{0:T(1024)} %multiply_bitcast_fusion.idx, bf16[16,512,512]{2,1,0:T(8,128)(2,1)} %tabs_hbm.1), custom_call_target="tpu_custom_call" | custom-call | tf_op jit(solution)/shard_map/pallas_call | solution.py:218
  48.8 1.3 %reduce_max.9 = s32[]{:T(128)} reduce(s32[8,256]{1,0:T(8,128)} %get-tuple-element.524, s32[]{:T(128)} %constant.378.clone.1), dimensions={0,1}, to_apply=%region_0.0 | reduce | flops 2047 | bytes 8200 | tf_op jit(solution)/shard_map/reduce_max | solution.py:312
  50.8 0.0 copy-done
  50.8 0.0 copy-start.1
  50.9 1.8 %add_dynamic-update-slice_fusion = f32[1024,512]{1,0:T(8,128)} fusion(f32[1024,512]{1,0:T(8,128)} %get-tuple-element.523, f32[128,512]{1,0:T(8,128)} %get-tuple-element.846), kind=kLoop, calls=%fused_computation.56 | loop fusion | flops 65536 | bytes 786432 | tf_op jit(solution)/shard_map/scatter-add | solution.py:316
  52.6 0.0 copy-done.1
  52.6 3.1 %broadcast_multiply_fusion = f32[1024,512]{1,0:T(8,128)} fusion(f32[1024,512]{1,0:T(8,128)} %add_dynamic-update-slice_fusion, f32[1024]{0:T(1024)S(1)} %convert_power_fusion), kind=kLoop, calls=%fused_computation.55 | loop fusion | flops 524288 | bytes 4198400 | tf_op jit(solution)/shard_map/mul | solution.py:318
  (2 shorter events, 0.0 us)
Async XLA Ops:
  1.4 49.4 %copy-start = (s32[3,256]{1,0:T(4,128)S(1)}, s32[3,256]{1,0:T(4,128)}, u32[]{:S(2)}) copy-start(s32[3,256]{1,0:T(4,128)} %pairs.1) | copy-start | bytes 9220
  50.8 1.8 %copy-start.1 = (s32[1024]{0:T(1024)S(1)}, s32[1024]{0:T(1024)}, u32[]{:S(2)}) copy-start(s32[1024]{0:T(1024)} %param.20) | copy-start | bytes 12292

commit v3 on v2

--- a/solution.py
+++ b/solution.py
@@ -10,6 +10,7 @@
 MESH = pl.DeviceIdType.MESH
 ROWS = 4
 ROOM = 64
+FIRST = 10
 STEPS = [(dx, dy) for dx in (-1, 0, 1) for dy in (-1, 0, 1) if (dx, dy) != (0, 0)]
 
 
@@ -39,16 +40,18 @@
     size_y,
     coef,
     pairs,
+    level,
     idx,
     tabs_hbm,
-    out,
-    border_out,
+    out_hbm,
+    inner_out,
     most_out,
     halo_out,
     lists_out,
     tabs,
     y,
     acc,
+    out,
     halo,
     lists,
     g,
@@ -61,6 +64,7 @@
     send_sem,
     recv_sem,
     save_sem,
+    out_sem,
 ):
     leaf_dev, width = coef.shape
     classes = tabs.shape[0]
@@ -80,6 +84,20 @@
     barrier = pltpu.get_barrier_semaphore()
     for dx, dy in STEPS:
         pl.semaphore_signal(barrier, inc=1, device_id=neighbour(dx, dy), device_id_type=MESH)
+    def tables_step(i, _):
+        for u in range(2):
+            c = i * 2 + u
+            table_copy(c).wait()
+            half = leaf_dev // 2
+            for m in range(0, leaf_dev, half):
+                r = dot(coef[m : m + half, :], tabs[c])
+                for j in range(ROWS):
+                    y[pl.ds(c * (ROWS * leaf_dev) + (ROWS * m + j), half, stride=ROWS), :] = r[
+                        :, 128 * j : 128 * j + 128
+                    ]
+        return 0
+
+    lax.fori_loop(0, FIRST // 2, tables_step, 0)
     pl.semaphore_wait(barrier, len(STEPS))
     copies = []
     for there, (dx, dy) in enumerate(STEPS):
@@ -98,30 +116,45 @@
             copy.start()
             copies.append(copy)
 
-    def tables_step(i, _):
-        for u in range(2):
-            c = i * 2 + u
-            table_copy(c).wait()
-            half = leaf_dev // 2
-            for m in range(0, leaf_dev, half):
-                r = dot(coef[m : m + half, :], tabs[c])
-                for j in range(ROWS):
-                    y[pl.ds(c * (ROWS * leaf_dev) + (ROWS * m + j), half, stride=ROWS), :] = r[
-                        :, 128 * j : 128 * j + 128
-                    ]
+    lax.fori_loop(FIRST // 2, classes // 2, tables_step, 0)
+
+    unroll = 8
+
+    def leaf_step(i, _):
+        first = (i // 16) * 1024 + (i % 16) * unroll
+        for u in range(unroll):
+            total = None
+            for k in range(8):
+                r = idx[first + (k * 128 + u)]
+                v = y[pl.ds(r, ROWS), :]
+                total = v if total is None else total + v
+            acc[pl.ds(i * (unroll * ROWS) + u * ROWS, ROWS), :] = total
         return 0
 
-    lax.fori_loop(0, classes // 2, tables_step, 0)
-
-    for copy in copies:
+    lax.fori_loop(0, leaf_dev // unroll, leaf_step, 0)
+
+    levels = level[...]
+    scale = jnp.ones(levels.shape, jnp.float32)
+    for bit in range(3):
+        scale = scale * jnp.where((levels & (1 << bit)) != 0, 0.25 ** (1 << bit), 1.0)
+
+    def scales(a):
+        return jnp.transpose(jnp.broadcast_to(scale[a : a + 1, :], (128, 128)))
+
+    for a in range(leaf_dev // 128):
+        by = scales(a)
+        for j in range(ROWS):
+            rows = acc[pl.ds(a * 128 * ROWS + j, 128, stride=ROWS), :] * by
+            out[a * 128 : a * 128 + 128, 128 * j : 128 * j + 128] = rows
+    rest_copy = pltpu.make_async_copy(
+        out.at[pl.ds(border, leaf_dev - border)],
+        out_hbm.at[pl.ds(border, leaf_dev - border)],
+        out_sem.at[0],
+    )
+    rest_copy.start()
+
+    for copy in copies[0::2]:
         copy.wait()
-    saves = [
-        pltpu.make_async_copy(halo, halo_out, save_sem.at[0]),
-        pltpu.make_async_copy(lists, lists_out, save_sem.at[1]),
-    ]
-    for save in saves:
-        save.start()
-
     target, source, kind = pairs[0:1, :], pairs[1:2, :], pairs[2:3, :]
     rank = my_x * size_y + my_y
     home = source // leaf_dev
@@ -133,7 +166,6 @@
     row_col = columns[:, 0:1].astype(jnp.int32)
     kind_col = columns[:, 1:2].astype(jnp.int32)
     picker = one_hot(iota((own, halo.shape[0]), 1) == row_col)
-    x_f[...] = dot(picker, halo[...]).astype(jnp.bfloat16)
 
     slots = classes * ROOM
     earlier = one_hot(iota((own, own), 0) < iota((own, own), 1))
@@ -168,11 +200,21 @@
         list_step,
         (jnp.zeros((classes, 1), jnp.float32), jnp.zeros((1, own), jnp.int32)),
     )
-    most_out[...] = jnp.broadcast_to(most, most_out.shape)
+    most_out[0] = jnp.max(most)
+    to_target = one_hot(iota((border, own), 0) == target - rank * leaf_dev)
+    to_source = jnp.transpose(back[...]).astype(jnp.bfloat16)
+    for copy in copies[1::2]:
+        copy.wait()
+    saves = [
+        pltpu.make_async_copy(halo, halo_out, save_sem.at[0]),
+        pltpu.make_async_copy(lists, lists_out, save_sem.at[1]),
+    ]
+    for save in saves:
+        save.start()
+    x_f[...] = dot(picker, halo[...]).astype(jnp.bfloat16)
     x_m[...] = dot(g[...], halo[...]).astype(jnp.bfloat16)
     z_f[...] = jnp.zeros_like(z_f)
 
-    share = leaf_dev // classes
 
     def class_step(c, _):
         table = tabs[c]
@@ -180,33 +222,29 @@
         z_f[...] += dot(rows, table)
         at = pl.ds(pl.multiple_of(c * ROOM, ROOM), ROOM)
         z_m[at, :] = dot_t(x_m[at, :], table)
-        first = (c // 2) * 1024 + (c % 2) * share
-        for u in range(share):
-            total = None
-            for k in range(8):
-                r = idx[first + (k * 128 + u)]
-                v = y[pl.ds(r, ROWS), :]
-                total = v if total is None else total + v
-            acc[pl.ds(pl.multiple_of(c * (share * ROWS) + u * ROWS, ROWS), ROWS), :] = total
         return 0
 
     lax.fori_loop(0, classes, class_step, 0)
 
-    to_target = one_hot(iota((border, own), 0) == target - rank * leaf_dev)
-    to_source = jnp.transpose(back[...]).astype(jnp.bfloat16)
     border_sum = None
     for picks, z in ((to_target, z_f[...]), (to_source, z_m[...])):
         for part in split(z):
             term = dot(picks, part)
             border_sum = term if border_sum is None else border_sum + term
-    border_out[...] = border_sum
+    inner_out[...] = out[0:border, :]
+    by = scales(0)
     for j in range(ROWS):
-        out[:, 128 * j : 128 * j + 128] = acc[pl.ds(j, leaf_dev, stride=ROWS), :]
-    for save in saves:
+        lanes = slice(128 * j, 128 * j + 128)
+        out[0:border, lanes] = out[0:border, lanes] + border_sum[:, lanes] * by
+    border_copy = pltpu.make_async_copy(
+        out.at[pl.ds(0, border)], out_hbm.at[pl.ds(0, border)], out_sem.at[1]
+    )
+    border_copy.start()
+    for save in (*saves, rest_copy, border_copy):
         save.wait()
 
 
-def near_parts(size_x, size_y, coef, tables, pairs, rows):
+def near_parts(size_x, size_y, coef, tables, pairs, level, rows):
     leaf_dev, width = coef.shape
     classes = tables.shape[0]
     border = leaf_dev // 8
@@ -215,21 +253,23 @@
     slots = classes * ROOM
     vmem = pl.BlockSpec(memory_space=pltpu.VMEM)
     hbm = pl.BlockSpec(memory_space=pl.ANY)
+    smem = pl.BlockSpec(memory_space=pltpu.SMEM)
     return pl.pallas_call(
         functools.partial(near_kernel, size_x, size_y),
         out_shape=(
             jax.ShapeDtypeStruct((leaf_dev, width), jnp.float32),
             jax.ShapeDtypeStruct((border, width), jnp.float32),
-            jax.ShapeDtypeStruct((8, own), jnp.int32),
+            jax.ShapeDtypeStruct((1,), jnp.int32),
             jax.ShapeDtypeStruct((places * border, width), jnp.bfloat16),
             jax.ShapeDtypeStruct((places, *pairs.shape), jnp.int32),
         ),
-        in_specs=[vmem, vmem, pl.BlockSpec(memory_space=pltpu.SMEM), hbm],
-        out_specs=(vmem, vmem, vmem, hbm, hbm),
+        in_specs=[vmem, vmem, vmem, smem, hbm],
+        out_specs=(hbm, vmem, smem, hbm, hbm),
         scratch_shapes=[
             pltpu.VMEM((classes, width, width), jnp.bfloat16),
             pltpu.VMEM((classes * leaf_dev * ROWS, 128), jnp.float32),
             pltpu.VMEM((leaf_dev * ROWS, 128), jnp.float32),
+            pltpu.VMEM((leaf_dev, width), jnp.float32),
             pltpu.VMEM((places * border, width), jnp.bfloat16),
             pltpu.VMEM((places, *pairs.shape), jnp.int32),
             pltpu.VMEM((slots, places * border), jnp.bfloat16),
@@ -242,11 +282,12 @@
             pltpu.SemaphoreType.DMA((2, places)),
             pltpu.SemaphoreType.DMA((2, places)),
             pltpu.SemaphoreType.DMA((2,)),
+            pltpu.SemaphoreType.DMA((2,)),
         ],
         compiler_params=pltpu.CompilerParams(
             collective_id=0, has_side_effects=True, vmem_limit_bytes=60 << 20
         ),
-    )(coef, pairs, rows, tables)
+    )(coef, pairs, level, rows, tables)
 
 
 def add_rows(index, count, values, valid):
@@ -305,17 +346,17 @@
     rank = lax.axis_index("gx") * size_y + lax.axis_index("gy")
     rows = (inner_class * leaf_dev + (inner_list - rank * leaf_dev)).T * ROWS
     rows = rows.reshape(knear, leaf_dev // 128, 128).transpose(1, 0, 2).reshape(-1)
-    near, border_sum, most, halo, lists = near_parts(
-        size_x, size_y, coef, tables, cross_pairs, rows
-    )
-    border_sum = lax.cond(
-        jnp.max(most) >= ROOM,
-        lambda: general_border(size_x, size_y, leaf_dev, halo, lists, cross_pairs, tables),
-        lambda: border_sum,
-    )
-    near = near.at[:border].add(border_sum)
-    scale = jnp.power(jnp.float32(0.25), leaf_level.astype(jnp.float32))
-    return near * scale[:, None]
+    level = leaf_level.reshape(leaf_dev // 128, 128)
+    out, inner, most, halo, lists = near_parts(
+        size_x, size_y, coef, tables, cross_pairs, level, rows
+    )
+
+    def general(out):
+        border_sum = general_border(size_x, size_y, leaf_dev, halo, lists, cross_pairs, tables)
+        scale = jnp.power(jnp.float32(0.25), leaf_level[:border].astype(jnp.float32))
+        return out.at[:border].set(inner + border_sum * scale[:, None])
+
+    return lax.cond(most[0] >= ROOM, general, lambda out: out, out)
 
 
 def solution(mesh):

time: 56.1 us -> 46.8 us (0.83)
  the two profiles are of different devices: /device:TPU:1 before, /device:TPU:61 now
where the time goes in v3:
time: 46.8 us; the launch traced here: 46.5 us
  Pallas kernels  41.4 us (88%)
  local copies, waits for them, and re-layouts  3.08 us (7%)
  other arithmetic  1.4 us (3%)
  between operations  0.7 us (1%)
    pallas_call x1, Pallas kernels, near_parts(): pl.pallas_call(functools.partial(near_kernel, size_x, size_y), out_shape=...  41.4 us
    unnamed x3, local copies, waits for them, and re-layouts  3.08 us
    reshape x1, other arithmetic, body(): rows.reshape(knear, leaf_dev // 128, 128).transpose(1, 0, 2).reshape(-1)  1.4 us

profile of v3, /device:TPU:61, one launch (start us, length us, event | category | flops | bytes accessed | tf_op | source)
XLA Modules:
  0.0 46.5 jit_solution(5444196430594867040)
XLA Ops:
  0.0 1.4 %multiply_bitcast_fusion.idx = s32[8192]{0:T(1024)} fusion(s32[1024,8]{0,1:T(8,128)} %param.21, s32[1024,8]{0,1:T(8,128)} %param.22, s32[]{:T(128)S(6)} %mul.93), kind=kLoop, calls=%fused_computation.57 | loop fusion | flops 32768 | bytes 98308 | tf_op jit(solution)/shard_map/reshape | solution.py:348
  1.4 0.0 copy-start
  1.4 41.4 %shard_map.66 = (f32[1024,512]{1,0:T(8,128)}, f32[128,512]{1,0:T(8,128)S(1)}, s32[1]{0:T(128)}, bf16[1024,512]{1,0:T(8,128)(2,1)S(1)}, s32[8,3,256]{2,1,0:T(4,128)S(1)}) custom-call(bf16[1024,512]{1,0:T(8,128)(2,1)} %coef.1, s32[3,256]{1,0:T(4,128)} %pairs.1, s32[8,128]{1,0:T(8,128)} %bitcast.42, s32[8192]{0:T(1024)} %multiply_bitcast_fusion.idx, ...), custom_call_target="tpu_custom_call" | custom-call | tf_op jit(solution)/shard_map/pallas_call | solution.py:257
  43.4 0.0 copy-done
  43.5 3.1 %copy.33 = f32[1024,512]{1,0:T(8,128)} copy(f32[1024,512]{1,0:T(8,128)} %get-tuple-element.537) | data formatting | bytes 4194304
  (1 shorter events, 0.0 us)
Async XLA Ops:
  1.4 42.0 %copy-start = (s32[3,256]{1,0:T(4,128)S(1)}, s32[3,256]{1,0:T(4,128)}, u32[]{:S(2)}) copy-start(s32[3,256]{1,0:T(4,128)} %pairs.1) | copy-start | bytes 9220

commit v4 on v3

v4 whole, which is shorter than its diff:
```python
import functools

import jax
import jax.numpy as jnp
from jax import lax
from jax.experimental import pallas as pl
from jax.experimental.pallas import tpu as pltpu
from jax.sharding import PartitionSpec as P

MESH = pl.DeviceIdType.MESH
ROWS = 4
ROOM = 64
FIRST = 8
SLOTS = 4
STEPS = [(-1, -1), (-1, 0), (-1, 1), (1, -1), (1, 0), (1, 1), (0, -1), (0, 1)]


def place_of(dx, dy):
    if isinstance(dx, int):
        return {-1: dy + 1, 1: dy + 4, 0: 6 + (dy + 1) // 2}[dx]
    return jnp.where(dx < 0, dy + 1, jnp.where(dx > 0, dy + 4, 6 + (dy + 1) // 2))


def dot(a, b):
    return jnp.dot(a, b, preferred_element_type=jnp.float32)


def dot_t(a, b):
    return lax.dot_general(a, b, (((1,), (1,)), ((), ())), preferred_element_type=jnp.float32)


def split(z):
    high = z.astype(jnp.bfloat16)
    return high, (z - high.astype(jnp.float32)).astype(jnp.bfloat16)


def one_hot(mask):
    return jnp.where(mask, 1.0, 0.0).astype(jnp.bfloat16)


def iota(shape, dim):
    return lax.broadcasted_iota(jnp.int32, shape, dim)


def scale_of(levels):
    scale = jnp.ones(levels.shape, jnp.float32)
    for bit in range(3):
        scale = scale * jnp.where((levels & (1 << bit)) != 0, 0.25 ** (1 << bit), 1.0)
    return scale


def down(scale, a):
    return jnp.transpose(jnp.broadcast_to(scale[a : a + 1, :], (128, 128)))


def near_kernel(
    size_x,
    size_y,
    coef,
    pairs,
    level,
    inner_list,
    inner_class,
    tabs_hbm,
    rest_out,
    border_out,
    inner_out,
    most_out,
    halo_out,
    lists_out,
    tabs,
    y,
    acc,
    out,
    idx,
    idx_slot,
    halo,
    lists,
    g,
    back,
    x_m,
    x_f,
    z_m,
    z_f,
    tab_sem,
    send_sem,
    recv_sem,
    save_sem,
    out_sem,
    idx_sem,
):
    leaf_dev, width = coef.shape
    classes = tabs.shape[0]
    border = leaf_dev // 8
    own = pairs.shape[1]
    my_x, my_y = lax.axis_index("gx"), lax.axis_index("gy")

    def table_copy(c):
        return pltpu.make_async_copy(tabs_hbm.at[c], tabs.at[c], tab_sem.at[c])

    for c in range(classes):
        table_copy(c).start()

    def neighbour(dx, dy):
        return lax.rem(my_x + dx + size_x, size_x), lax.rem(my_y + dy + size_y, size_y)

    barrier = pltpu.get_barrier_semaphore()
    for dx, dy in STEPS:
        pl.semaphore_signal(barrier, inc=1, device_id=neighbour(dx, dy), device_id_type=MESH)
    idx[...] = ((inner_class[...] & (classes - 1)) * leaf_dev + (inner_list[...] & (leaf_dev - 1))) * ROWS

    def idx_copy(chunk, slot):
        lanes = pl.ds(pl.multiple_of(chunk * 128, 128), 128)
        return pltpu.make_async_copy(idx.at[:, lanes], idx_slot.at[slot], idx_sem.at[slot])

    def tables_step(i, _):
        for u in range(2):
            c = i * 2 + u
            table_copy(c).wait()
            half = leaf_dev // 2
            for m in range(0, leaf_dev, half):
                r = dot(coef[m : m + half, :], tabs[c])
                for j in range(ROWS):
                    y[pl.ds(c * (ROWS * leaf_dev) + (ROWS * m + j), half, stride=ROWS), :] = r[
                        :, 128 * j : 128 * j + 128
                    ]
        return 0

    lax.fori_loop(0, FIRST // 2, tables_step, 0)
    pl.semaphore_wait(barrier, len(STEPS))
    mate = 1 - 2 * lax.rem(my_y, 2)

    def rows_of(place):
        return halo.at[pl.ds(place * border, border)]

    def halo_copy(source, sent, place, dx, dy):
        return pltpu.make_async_remote_copy(
            src_ref=source,
            dst_ref=rows_of(place),
            send_sem=send_sem.at[0, sent],
            recv_sem=recv_sem.at[0, place],
            device_id=neighbour(dx, dy),
            device_id_type=MESH,
        )

    list_copies = []
    for there, (dx, dy) in enumerate(STEPS):
        copy = pltpu.make_async_remote_copy(
            src_ref=pairs,
            dst_ref=lists.at[place_of(-dx, -dy)],
            send_sem=send_sem.at[1, there],
            recv_sem=recv_sem.at[1, place_of(-dx, -dy)],
            device_id=neighbour(dx, dy),
            device_id_type=MESH,
        )
        copy.start()
        list_copies.append(copy)
    mine = coef.at[pl.ds(0, border)]
    sends = [(0, -mate), (-1, -mate), (1, -mate), (-1, 0), (1, 0), (0, mate)]
    halo_copies = [
        halo_copy(mine, sent, place_of(-dx, -dy), dx, dy) for sent, (dx, dy) in enumerate(sends)
    ]
    for copy in halo_copies:
        copy.start()
    for slot in range(SLOTS):
        idx_copy(slot, slot).start()
    lax.fori_loop(FIRST // 2, classes // 2, tables_step, 0)

    def leaf_step(i, _):
        for slot in range(SLOTS):
            chunk = i * SLOTS + slot
            idx_copy(chunk, slot).wait()
            for u in range(128):
                total = None
                for k in range(8):
                    v = y[pl.ds(idx_slot[slot, k, u], ROWS), :]
                    total = v if total is None else total + v
                acc[pl.ds(chunk * (128 * ROWS) + u * ROWS, ROWS), :] = total

            idx_copy(lax.rem(chunk + SLOTS, leaf_dev // 128), slot).start()
        return 0

    lax.fori_loop(0, leaf_dev // 128 // SLOTS, leaf_step, 0)
    for slot in range(SLOTS):
        idx_copy(slot, slot).wait()

    scale = scale_of(level[...])

    for a in range(leaf_dev // 128):
        by = down(scale, a)
        for j in range(ROWS):
            rows = acc[pl.ds(a * 128 * ROWS + j, 128, stride=ROWS), :] * by
            out[a * 128 : a * 128 + 128, 128 * j : 128 * j + 128] = rows
    rest_copy = pltpu.make_async_copy(
        out.at[pl.ds(border, leaf_dev - border)], rest_out, out_sem.at[0]
    )
    rest_copy.start()

    for sent, dx in ((6, -1), (7, 1)):
        came = place_of(dx, 0)
        halo_copy(rows_of(came), sent, came, 0, mate).wait_recv()
        copy = halo_copy(rows_of(came), sent, place_of(dx, -mate), 0, mate)
        copy.start()
        halo_copies.append(copy)
    for copy in list_copies:
        copy.wait()
    target, source, kind = pairs[0:1, :], pairs[1:2, :], pairs[2:3, :]
    rank = my_x * size_y + my_y
    home = source // leaf_dev
    place = place_of(home // size_y - my_x, home % size_y - my_y)
    row = place * border + source % leaf_dev
    line = iota((128, own), 0)
    columns = jnp.transpose(jnp.where(line == 0, row, kind).astype(jnp.float32))
    row_col = columns[:, 0:1].astype(jnp.int32)
    kind_col = columns[:, 1:2].astype(jnp.int32)
    picker = one_hot(iota((own, halo.shape[0]), 1) == row_col)

    slots = classes * ROOM
    earlier = one_hot(iota((own, own), 0) < iota((own, own), 1))
    back[...] = jnp.zeros_like(back)

    def list_step(o, carry):
        before, most = carry
        from_leaf = lists[o, 0:1, :] % leaf_dev
        to_leaf = lists[o, 1:2, :] - rank * leaf_dev
        o_kind = lists[o, 2:3, :]
        here = (to_leaf >= 0) & (to_leaf < border)
        kinds = one_hot((iota((classes, own), 0) == o_kind) & here)
        ahead = dot(kinds, earlier) + before
        hits = kinds.astype(jnp.float32)
        place_in = jnp.sum(ahead * hits, axis=0, keepdims=True).astype(jnp.int32)
        most = jnp.maximum(most, jnp.where(here, place_in, 0))
        room = one_hot(iota((ROOM, own), 0) == place_in)
        e = jnp.concatenate([room * kinds[c : c + 1, :] for c in range(classes)], axis=0)
        lines = iota((2 * border, own), 0)
        w = one_hot(lines == jnp.where(lines < border, from_leaf, to_leaf + border))
        both = dot_t(e, w)
        g[:, pl.ds(pl.multiple_of(o * border, border), border)] = both[:, :border].astype(jnp.bfloat16)
        back[...] += both[:, border:]
        return before + jnp.sum(hits, axis=1, keepdims=True), most

    _, most = lax.fori_loop(
        0,
        len(STEPS),
        list_step,
        (jnp.zeros((classes, 1), jnp.float32), jnp.zeros((1, own), jnp.int32)),
    )
    most_out[0] = jnp.max(most)
    to_target = one_hot(iota((border, own), 0) == target - rank * leaf_dev)
    to_source = jnp.transpose(back[...]).astype(jnp.bfloat16)
    for copy in halo_copies:
        copy.wait_send()
    for place in range(len(STEPS)):
        if place not in (place_of(-1, 0), place_of(1, 0)):
            halo_copy(rows_of(place), 0, place, 0, mate).wait_recv()
    saves = [
        pltpu.make_async_copy(halo, halo_out.at[pl.ds(0, halo.shape[0])], save_sem.at[0]),
        pltpu.make_async_copy(lists, lists_out, save_sem.at[1]),
    ]
    for save in saves:
        save.start()
    x_f[...] = dot(picker, halo[...]).astype(jnp.bfloat16)
    x_m[...] = dot(g[...], halo[...]).astype(jnp.bfloat16)


    for c in range(classes):
        rows = jnp.where(kind_col == c, x_f[...].astype(jnp.float32), 0.0).astype(jnp.bfloat16)
        part = dot(rows, tabs[c])
        z_f[...] = part if c == 0 else z_f[...] + part
        z_m[c * ROOM : (c + 1) * ROOM, :] = dot_t(x_m[c * ROOM : (c + 1) * ROOM, :], tabs[c])

    border_sum = None
    for picks, z in ((to_target, z_f[...]), (to_source, z_m[...])):
        for part in split(z):
            term = dot(picks, part)
            border_sum = term if border_sum is None else border_sum + term
    inner_out[...] = out[0:border, :]
    by = down(scale, 0)
    for j in range(ROWS):
        lanes = slice(128 * j, 128 * j + 128)
        border_out[:, lanes] = out[0:border, lanes] + border_sum[:, lanes] * by
    for save in (*saves, rest_copy):
        save.wait()


def near_parts(size_x, size_y, coef, tables, pairs, level, inner_list, inner_class):
    leaf_dev, width = coef.shape
    classes = tables.shape[0]
    border = leaf_dev // 8
    own = pairs.shape[1]
    places = len(STEPS)
    slots = classes * ROOM
    vmem = pl.BlockSpec(memory_space=pltpu.VMEM)
    hbm = pl.BlockSpec(memory_space=pl.ANY)
    smem = pl.BlockSpec(memory_space=pltpu.SMEM)
    return pl.pallas_call(
        functools.partial(near_kernel, size_x, size_y),
        out_shape=(
            jax.ShapeDtypeStruct((leaf_dev - border, width), jnp.float32),
            jax.ShapeDtypeStruct((border, width), jnp.float32),
            jax.ShapeDtypeStruct((border, width), jnp.float32),
            jax.ShapeDtypeStruct((1,), jnp.int32),
            jax.ShapeDtypeStruct((12 * places * border, width), jnp.bfloat16),
            jax.ShapeDtypeStruct((places, *pairs.shape), jnp.int32),
        ),
        in_specs=[vmem, vmem, vmem, vmem, vmem, hbm],
        out_specs=(hbm, vmem, vmem, smem, hbm, hbm),
        scratch_shapes=[
            pltpu.VMEM((classes, width, width), jnp.bfloat16),
            pltpu.VMEM((classes * leaf_dev * ROWS, 128), jnp.float32),
            pltpu.VMEM((leaf_dev * ROWS, 128), jnp.float32),
            pltpu.VMEM((leaf_dev, width), jnp.float32),
            pltpu.VMEM(inner_list.shape, jnp.int32),
            pltpu.SMEM((SLOTS, inner_list.shape[0], 128), jnp.int32),
            pltpu.VMEM((places * border, width), jnp.bfloat16),
            pltpu.VMEM((places, *pairs.shape), jnp.int32),
            pltpu.VMEM((slots, places * border), jnp.bfloat16),
            pltpu.VMEM((slots, border), jnp.float32),
            pltpu.VMEM((slots, width), jnp.bfloat16),
            pltpu.VMEM((own, width), jnp.bfloat16),
            pltpu.VMEM((slots, width), jnp.float32),
            pltpu.VMEM((own, width), jnp.float32),
            pltpu.SemaphoreType.DMA((classes,)),
            pltpu.SemaphoreType.DMA((2, places)),
            pltpu.SemaphoreType.DMA((2, places)),
            pltpu.SemaphoreType.DMA((2,)),
            pltpu.SemaphoreType.DMA((1,)),
            pltpu.SemaphoreType.DMA((SLOTS,)),
        ],
        compiler_params=pltpu.CompilerParams(
            collective_id=0, has_side_effects=True, vmem_limit_bytes=54 << 20
        ),
    )(coef, pairs, level, inner_list, inner_class, tables)


def finish_kernel(
    size_x,
    size_y,
    most,
    rest,
    fast,
    inner,
    halo_hbm,
    lists_hbm,
    pairs_hbm,
    level_hbm,
    tabs_hbm,
    out,
    halo,
    lists,
    pairs,
    level,
    table,
    total,
    final,
    whole,
    sem,
):
    border, width = total.shape
    own = pairs.shape[1]
    leaf_dev = out.shape[0]
    pieces = leaf_dev // border

    def piece(i):
        return pl.ds(i * border, border)

    taken = [
        pltpu.make_async_copy(rest.at[piece(i - 1)] if i else fast, whole.at[piece(i)], sem.at[0, i])
        for i in range(pieces)
    ]
    given = [pltpu.make_async_copy(whole.at[piece(i)], out.at[piece(i)], sem.at[1, i]) for i in range(pieces)]
    for copy in taken:
        copy.start()
    for copy, onward in zip(taken, given, strict=True):
        copy.wait()
        onward.start()
    for copy in given:
        copy.wait()

    @pl.when(most[0] >= ROOM)
    def _():
        def bring(source, target):
            copy = pltpu.make_async_copy(source, target, sem.at[0, 0])
            copy.start()
            copy.wait()

        bring(halo_hbm.at[pl.ds(0, halo.shape[0])], halo)
        bring(lists_hbm, lists)
        bring(pairs_hbm, pairs)
        bring(level_hbm, level)
        my_x, my_y = lax.axis_index("gx"), lax.axis_index("gy")
        rank = my_x * size_y + my_y

        def add(row, kind, at, times):
            line = iota((128, own), 0)
            columns = jnp.transpose(jnp.where(line == 0, row, kind).astype(jnp.float32))
            row_col = columns[:, 0:1].astype(jnp.int32)
            kind_col = columns[:, 1:2].astype(jnp.int32)
            rows = dot(one_hot(iota((own, halo.shape[0]), 1) == row_col), halo[...])
            picks = one_hot(iota((border, own), 0) == at)

            def class_step(c, _):
                bring(tabs_hbm.at[c], table)
                for part in split(times(jnp.where(kind_col == c, rows, 0.0).astype(jnp.bfloat16), table[...])):
                    total[...] += dot(picks, part)
                return 0

            lax.fori_loop(0, tabs_hbm.shape[0], class_step, 0)

        total[...] = jnp.zeros_like(total)
        target, source, kind = pairs[0:1, :], pairs[1:2, :], pairs[2:3, :]
        home = source // leaf_dev
        place = place_of(home // size_y - my_x, home % size_y - my_y)
        add(place * border + source % leaf_dev, kind, target - rank * leaf_dev, dot)

        def list_step(o, _):
            row = o * border + lists[o, 0:1, :] % leaf_dev
            add(row, lists[o, 2:3, :], lists[o, 1:2, :] - rank * leaf_dev, dot_t)
            return 0

        lax.fori_loop(0, lists.shape[0], list_step, 0)
        bring(inner, final)
        by = down(scale_of(level[...]), 0)
        for j in range(width // 128):
            lanes = slice(128 * j, 128 * j + 128)
            final[:, lanes] = final[:, lanes] + total[:, lanes] * by
        bring(final, out.at[pl.ds(0, border)])


def finish(size_x, size_y, most, rest, fast, inner, halo, lists, pairs, level, tables):
    border, width = fast.shape
    hbm = pl.BlockSpec(memory_space=pl.ANY)
    return pl.pallas_call(
        functools.partial(finish_kernel, size_x, size_y),
        out_shape=jax.ShapeDtypeStruct((rest.shape[0] + border, width), jnp.float32),
        in_specs=[pl.BlockSpec(memory_space=pltpu.SMEM)] + [hbm] * 8,
        out_specs=hbm,
        scratch_shapes=[
            pltpu.VMEM((len(STEPS) * border, width), jnp.bfloat16),
            pltpu.VMEM(lists.shape, jnp.int32),
            pltpu.VMEM(pairs.shape, jnp.int32),
            pltpu.VMEM(level.shape, jnp.int32),
            pltpu.VMEM(tables.shape[1:], jnp.bfloat16),
            pltpu.VMEM((border, width), jnp.float32),
            pltpu.VMEM((border, width), jnp.float32),
            pltpu.VMEM((rest.shape[0] + border, width), jnp.float32),
            pltpu.SemaphoreType.DMA((2, rest.shape[0] // border + 1)),
        ],
        compiler_params=pltpu.CompilerParams(vmem_limit_bytes=60 << 20),
    )(most, rest, fast, inner, halo, lists, pairs, level, tables)


def body(coef, tables, leaf_level, inner_list, inner_class, cross_pairs):
    leaf_dev, width = coef.shape
    size_x, size_y = lax.axis_size("gx"), lax.axis_size("gy")
    level = leaf_level.reshape(leaf_dev // 128, 128)
    rest, fast, inner, most, halo, lists = near_parts(
        size_x, size_y, coef, tables, cross_pairs, level, inner_list.T, inner_class.T
    )

    return finish(size_x, size_y, most, rest, fast, inner, halo, lists, cross_pairs, level, tables)


def solution(mesh):
    return jax.shard_map(
        body,
        mesh=mesh,
        in_specs=(
            P(("gx", "gy"), None),
            P(),
            P(("gx", "gy")),
            P(("gx", "gy"), None),
            P(("gx", "gy"), None),
            P(None, ("gx", "gy")),
        ),
        out_specs=P(("gx", "gy"), None),
        check_vma=False,
    )
```

time: 46.8 us -> 35.9 us (0.77)
  the two profiles are of different devices: /device:TPU:61 before, /device:TPU:1 now
where the time goes in v4:
time: 35.9 us; the launch traced here: 35.7 us
  Pallas kernels  35.7 us (99%)
    pallas_call x1, Pallas kernels, near_parts(): pl.pallas_call(functools.partial(near_kernel, size_x, size_y), out_shape=...  32.7 us
    pallas_call x1, Pallas kernels, finish(): pl.pallas_call(functools.partial(finish_kernel, size_x, size_y), out_shap...  3.08 us

profile of v4, /device:TPU:1, one launch (start us, length us, event | category | flops | bytes accessed | tf_op | source)
XLA Modules:
  0.0 35.7 jit_solution(5796048160890416016)
XLA Ops:
  0.0 32.7 %shard_map.64 = (f32[896,512]{1,0:T(8,128)}, f32[128,512]{1,0:T(8,128)}, f32[128,512]{1,0:T(8,128)}, s32[1]{0:T(128)}, bf16[12288,512]{1,0:T(8,128)(2,1)}, /*index=5*/s32[8,3,256]{2,1,0:T(4,128)}) custom-call(bf16[1024,512]{1,0:T(8,128)(2,1)} %coef.1, s32[3,256]{1,0:T(4,128)} %pairs_hbm.1, s32[8,128]{1,0:T(8,128)} %bitcast.5, s32[8,1024]{1,0:T(8,128)} %bitcast.3, ...), custom_call_target="tpu_custom_call" | custom-call | tf_op jit(solution)/shard_map/pallas_call | solution.py:296
  32.7 3.1 %shard_map.65 = f32[1024,512]{1,0:T(8,128)} custom-call(s32[1]{0:T(128)} %get-tuple-element.11.most, f32[896,512]{1,0:T(8,128)} %get-tuple-element.12.rest, f32[128,512]{1,0:T(8,128)} %get-tuple-element.13.fast, f32[128,512]{1,0:T(8,128)} %get-tuple-element.14.inner, bf16[12288,512]{1,0:T(8,128)(2,1)} %get-tuple-element.15.halo_hbm, ...), custom_call_target="tpu_custom_call" | custom-call | tf_op jit(solution)/shard_map/pallas_call | solution.py:433

commit v5 on v4

--- a/solution.py
+++ b/solution.py
@@ -10,7 +10,7 @@
 MESH = pl.DeviceIdType.MESH
 ROWS = 4
 ROOM = 64
-FIRST = 8
+FIRST = 6
 SLOTS = 4
 STEPS = [(-1, -1), (-1, 0), (-1, 1), (1, -1), (1, 0), (1, 1), (0, -1), (0, 1)]
 
@@ -56,11 +56,11 @@
 def near_kernel(
     size_x,
     size_y,
-    coef,
-    pairs,
-    level,
-    inner_list,
-    inner_class,
+    coef_hbm,
+    pairs_hbm,
+    level_hbm,
+    inner_list_hbm,
+    inner_class_hbm,
     tabs_hbm,
     rest_out,
     border_out,
@@ -68,6 +68,11 @@
     most_out,
     halo_out,
     lists_out,
+    coef,
+    pairs,
+    level,
+    inner_list,
+    inner_class,
     tabs,
     y,
     acc,
@@ -88,6 +93,7 @@
     save_sem,
     out_sem,
     idx_sem,
+    arg_sem,
 ):
     leaf_dev, width = coef.shape
     classes = tabs.shape[0]
@@ -98,7 +104,24 @@
     def table_copy(c):
         return pltpu.make_async_copy(tabs_hbm.at[c], tabs.at[c], tab_sem.at[c])
 
-    for c in range(classes):
+    arguments = [
+        pltpu.make_async_copy(source, target, arg_sem.at[i])
+        for i, (source, target) in enumerate(
+            (
+                (coef_hbm, coef),
+                (pairs_hbm, pairs),
+                (level_hbm, level),
+                (inner_list_hbm, inner_list),
+                (inner_class_hbm, inner_class),
+            )
+        )
+    ]
+    arguments[0].start()
+    for c in range(2):
+        table_copy(c).start()
+    for argument in arguments[1:]:
+        argument.start()
+    for c in range(2, classes):
         table_copy(c).start()
 
     def neighbour(dx, dy):
@@ -107,7 +130,6 @@
     barrier = pltpu.get_barrier_semaphore()
     for dx, dy in STEPS:
         pl.semaphore_signal(barrier, inc=1, device_id=neighbour(dx, dy), device_id_type=MESH)
-    idx[...] = ((inner_class[...] & (classes - 1)) * leaf_dev + (inner_list[...] & (leaf_dev - 1))) * ROWS
 
     def idx_copy(chunk, slot):
         lanes = pl.ds(pl.multiple_of(chunk * 128, 128), 128)
@@ -126,7 +148,10 @@
                     ]
         return 0
 
+    arguments[0].wait()
     lax.fori_loop(0, FIRST // 2, tables_step, 0)
+    for argument in arguments[1:]:
+        argument.wait()
     pl.semaphore_wait(barrier, len(STEPS))
     mate = 1 - 2 * lax.rem(my_y, 2)
 
@@ -156,12 +181,13 @@
         copy.start()
         list_copies.append(copy)
     mine = coef.at[pl.ds(0, border)]
-    sends = [(0, -mate), (-1, -mate), (1, -mate), (-1, 0), (1, 0), (0, mate)]
+    sends = [(-1, 0), (1, 0), (0, -mate), (-1, -mate), (1, -mate), (0, mate)]
     halo_copies = [
         halo_copy(mine, sent, place_of(-dx, -dy), dx, dy) for sent, (dx, dy) in enumerate(sends)
     ]
     for copy in halo_copies:
         copy.start()
+    idx[...] = ((inner_class[...] & (classes - 1)) * leaf_dev + (inner_list[...] & (leaf_dev - 1))) * ROWS
     for slot in range(SLOTS):
         idx_copy(slot, slot).start()
     lax.fori_loop(FIRST // 2, classes // 2, tables_step, 0)
@@ -219,8 +245,9 @@
     earlier = one_hot(iota((own, own), 0) < iota((own, own), 1))
     back[...] = jnp.zeros_like(back)
 
-    def list_step(o, carry):
-        before, most = carry
+    before = jnp.zeros((classes, 1), jnp.float32)
+    most = jnp.zeros((1, own), jnp.int32)
+    for o in range(len(STEPS)):
         from_leaf = lists[o, 0:1, :] % leaf_dev
         to_leaf = lists[o, 1:2, :] - rank * leaf_dev
         o_kind = lists[o, 2:3, :]
@@ -235,16 +262,9 @@
         lines = iota((2 * border, own), 0)
         w = one_hot(lines == jnp.where(lines < border, from_leaf, to_leaf + border))
         both = dot_t(e, w)
-        g[:, pl.ds(pl.multiple_of(o * border, border), border)] = both[:, :border].astype(jnp.bfloat16)
+        g[:, o * border : (o + 1) * border] = both[:, :border].astype(jnp.bfloat16)
         back[...] += both[:, border:]
-        return before + jnp.sum(hits, axis=1, keepdims=True), most
-
-    _, most = lax.fori_loop(
-        0,
-        len(STEPS),
-        list_step,
-        (jnp.zeros((classes, 1), jnp.float32), jnp.zeros((1, own), jnp.int32)),
-    )
+        before = before + jnp.sum(hits, axis=1, keepdims=True)
     most_out[0] = jnp.max(most)
     to_target = one_hot(iota((border, own), 0) == target - rank * leaf_dev)
     to_source = jnp.transpose(back[...]).astype(jnp.bfloat16)
@@ -303,9 +323,14 @@
             jax.ShapeDtypeStruct((12 * places * border, width), jnp.bfloat16),
             jax.ShapeDtypeStruct((places, *pairs.shape), jnp.int32),
         ),
-        in_specs=[vmem, vmem, vmem, vmem, vmem, hbm],
+        in_specs=[hbm] * 6,
         out_specs=(hbm, vmem, vmem, smem, hbm, hbm),
         scratch_shapes=[
+            pltpu.VMEM(coef.shape, coef.dtype),
+            pltpu.VMEM(pairs.shape, jnp.int32),
+            pltpu.VMEM(level.shape, jnp.int32),
+            pltpu.VMEM(inner_list.shape, jnp.int32),
+            pltpu.VMEM(inner_class.shape, jnp.int32),
             pltpu.VMEM((classes, width, width), jnp.bfloat16),
             pltpu.VMEM((classes * leaf_dev * ROWS, 128), jnp.float32),
             pltpu.VMEM((leaf_dev * ROWS, 128), jnp.float32),
@@ -326,6 +351,7 @@
             pltpu.SemaphoreType.DMA((2,)),
             pltpu.SemaphoreType.DMA((1,)),
             pltpu.SemaphoreType.DMA((SLOTS,)),
+            pltpu.SemaphoreType.DMA((5,)),
         ],
         compiler_params=pltpu.CompilerParams(
             collective_id=0, has_side_effects=True, vmem_limit_bytes=54 << 20

time: 35.9 us -> 34.4 us (0.958)
  Pallas kernels: 35.7 us -> 34.2 us
    pallas_call x1, Pallas kernels: 32.7 us -> 31.1 us  [near_parts(): pl.pallas_call(functools.partial(near_kernel, size_x, size_y), out_shape=...]
where the time goes in v5:
time: 34.4 us; the launch traced here: 34.2 us
  Pallas kernels  34.2 us (99%)
    pallas_call x1, Pallas kernels, near_parts(): pl.pallas_call(functools.partial(near_kernel, size_x, size_y), out_shape=...  31.1 us
    pallas_call x1, Pallas kernels, finish(): pl.pallas_call(functools.partial(finish_kernel, size_x, size_y), out_shap...  3.08 us

profile of v5, /device:TPU:1, one launch (start us, length us, event | category | flops | bytes accessed | tf_op | source)
XLA Modules:
  0.0 34.2 jit_solution(12629161897152547118)
XLA Ops:
  0.0 31.1 %shard_map.64 = (f32[896,512]{1,0:T(8,128)}, f32[128,512]{1,0:T(8,128)}, f32[128,512]{1,0:T(8,128)}, s32[1]{0:T(128)}, bf16[12288,512]{1,0:T(8,128)(2,1)}, /*index=5*/s32[8,3,256]{2,1,0:T(4,128)}) custom-call(bf16[1024,512]{1,0:T(8,128)(2,1)} %coef_hbm.1, s32[3,256]{1,0:T(4,128)} %pairs_hbm.3, s32[8,128]{1,0:T(8,128)} %bitcast.5, s32[8,1024]{1,0:T(8,128)} %bitcast.3, ...), custom_call_target="tpu_custom_call" | custom-call | tf_op jit(solution)/shard_map/pallas_call | solution.py:316
  31.1 3.1 %shard_map.65 = f32[1024,512]{1,0:T(8,128)} custom-call(s32[1]{0:T(128)} %get-tuple-element.11.most, f32[896,512]{1,0:T(8,128)} %get-tuple-element.12.rest, f32[128,512]{1,0:T(8,128)} %get-tuple-element.13.fast, f32[128,512]{1,0:T(8,128)} %get-tuple-element.14.inner, bf16[12288,512]{1,0:T(8,128)(2,1)} %get-tuple-element.15.halo_hbm, ...), custom_call_target="tpu_custom_call" | custom-call | tf_op jit(solution)/shard_map/pallas_call | solution.py:459

commit v6 on v5

--- a/solution.py
+++ b/solution.py
@@ -332,8 +332,8 @@
             pltpu.VMEM(inner_list.shape, jnp.int32),
             pltpu.VMEM(inner_class.shape, jnp.int32),
             pltpu.VMEM((classes, width, width), jnp.bfloat16),
-            pltpu.VMEM((classes * leaf_dev * ROWS, 128), jnp.float32),
-            pltpu.VMEM((leaf_dev * ROWS, 128), jnp.float32),
+            pltpu.VMEM((classes * leaf_dev * ROWS + 8, 128), jnp.float32),
+            pltpu.VMEM((leaf_dev * ROWS + 8, 128), jnp.float32),
             pltpu.VMEM((leaf_dev, width), jnp.float32),
             pltpu.VMEM(inner_list.shape, jnp.int32),
             pltpu.SMEM((SLOTS, inner_list.shape[0], 128), jnp.int32),

time: 34.4 us -> 34.4 us (level)
  no operation moved by 1% of the time
where the time goes in v6:
time: 34.4 us; the launch traced here: 34.2 us
  Pallas kernels  34.2 us (99%)
    pallas_call x1, Pallas kernels, near_parts(): pl.pallas_call(functools.partial(near_kernel, size_x, size_y), out_shape=...  31.1 us
    pallas_call x1, Pallas kernels, finish(): pl.pallas_call(functools.partial(finish_kernel, size_x, size_y), out_shap...  3.08 us

profile of v6, /device:TPU:1, one launch (start us, length us, event | category | flops | bytes accessed | tf_op | source)
XLA Modules:
  0.0 34.2 jit_solution(8189829245387127725)
XLA Ops:
  0.0 31.1 %shard_map.64 = (f32[896,512]{1,0:T(8,128)}, f32[128,512]{1,0:T(8,128)}, f32[128,512]{1,0:T(8,128)}, s32[1]{0:T(128)}, bf16[12288,512]{1,0:T(8,128)(2,1)}, /*index=5*/s32[8,3,256]{2,1,0:T(4,128)}) custom-call(bf16[1024,512]{1,0:T(8,128)(2,1)} %coef_hbm.1, s32[3,256]{1,0:T(4,128)} %pairs_hbm.3, s32[8,128]{1,0:T(8,128)} %bitcast.5, s32[8,1024]{1,0:T(8,128)} %bitcast.3, ...), custom_call_target="tpu_custom_call" | custom-call | tf_op jit(solution)/shard_map/pallas_call | solution.py:316
  31.1 3.1 %shard_map.65 = f32[1024,512]{1,0:T(8,128)} custom-call(s32[1]{0:T(128)} %get-tuple-element.11.most, f32[896,512]{1,0:T(8,128)} %get-tuple-element.12.rest, f32[128,512]{1,0:T(8,128)} %get-tuple-element.13.fast, f32[128,512]{1,0:T(8,128)} %get-tuple-element.14.inner, bf16[12288,512]{1,0:T(8,128)(2,1)} %get-tuple-element.15.halo_hbm, ...), custom_call_target="tpu_custom_call" | custom-call | tf_op jit(solution)/shard_map/pallas_call | solution.py:459
